TPU v7x, 256 devices: a whole 4x4x8 slice. The times are simulated.
256 devices in a mesh: prow: 16 (over x, y), pcol: 16 (over z, core).
Axes of the slice: x: 4, y: 4, z: 8, core: 2. Of those that a mesh axis runs over, the one named last changes fastest.
Arguments:
- left_factor: bfloat16 [64, 32, 2048, 128], P('prow', 'pcol'), may hold values from -0.8984375 to 0.8984375
- right_factor: bfloat16 [64, 32, 2048, 128], P('prow', 'pcol'), may hold values from -0.8984375 to 0.8984375
- pivot_left: bfloat16 [32, 2048, 128], P('pcol', 'prow'), may hold values from -0.8984375 to 0.8984375
- pivot_right: bfloat16 [32, 2048, 128], P('pcol', 'prow'), may hold values from -0.8984375 to 0.8984375
- target_left: bfloat16 [2048, 64, 128], P('pcol', 'prow'), may hold values from -6 to 6
- target_right: bfloat16 [2048, 64, 128], P('pcol', 'prow'), may hold values from -6 to 6
- probe: bfloat16 [2048, 128], P('prow'), may hold values from -6 to 6
- ranks: int32 [64, 32], P('prow', 'pcol'), may hold values from 16 to 128
Outputs:
- basis: float32 [2048, 64, 128], P('pcol', 'prow')
- coefficient: float32 [2048, 64, 128], P('pcol', 'prow')
All inputs are finite; a program needn't handle non-finite values.
Results may differ from a plain program's by a relative error of at most 0.0038.
Values may be sent and summed in bfloat16 or wider, within the bound.
No kernel may reach another device: no remote copies, remote signals or barrier semaphores. Data moves between devices by JAX's collectives and lax.ppermute only.
A program may use at most 64 MiB of HBM per device.

v0:
```python
import jax
import jax.numpy as jnp
from jax import lax
from jax.experimental import pallas as pl
from jax.experimental.pallas import tpu as pltpu
from jax.sharding import PartitionSpec as P


F32 = jnp.float32
BF = jnp.bfloat16
SIDE = 4
CHIPS = 8
CORES = 2
NB = 32


def dims(a, b, ca, cb, precision=None):
    return lax.dot_general(
        a, b, (((ca,), (cb,)), ((), ())), precision=precision, preferred_element_type=F32
    )


def halves(v):
    high = v.astype(BF)
    return high, (v - high.astype(F32)).astype(BF)


def fine(a, b, ca, cb):
    ah, al = halves(a)
    bh, bl = halves(b)
    return dims(ah, bh, ca, cb) + (dims(ah, bl, ca, cb) + dims(al, bh, ca, cb))


def to_sibling(v):
    return lax.ppermute(v, "pcol", [(i, i ^ 1) for i in range(CHIPS * CORES)])


def along_z(v, k):
    n = CHIPS * CORES
    return lax.ppermute(v, "pcol", [(i, (i + CORES * k) % n) for i in range(n)])


def along_y(v, d):
    return lax.ppermute(
        v, "prow", [(SIDE * x + y, SIDE * x + (y + d) % SIDE) for x in range(SIDE) for y in range(SIDE)]
    )


def along_x(v, d):
    return lax.ppermute(
        v, "prow", [(SIDE * x + y, SIDE * ((x + d) % SIDE) + y) for x in range(SIDE) for y in range(SIDE)]
    )


def first_stage(v, along):
    parts = [along(v, d) for d in (1, 2, -1)]
    return jnp.stack([v, *parts])


def second_stage(stacked, along, tag):
    far = along(stacked, -1)
    near = along(stacked, 1)
    if tag == "rights":
        return [stacked, near, along(stacked, 2), far]
    even = along(stacked[:, :1], 2)
    return [stacked, near, even, along(far[:, 1:], -1), far]


def gather_line(v):
    up = [v]
    down = [v]
    for step in range(CHIPS // 2):
        up.append(along_z(up[-1], 1))
        if step < CHIPS // 2 - 1:
            down.append(along_z(down[-1], -1))
    first = to_sibling(stack(up[0], up[1], up[2], down[1]))
    second = to_sibling(stack(down[2], down[3], up[3], up[4]))
    return up + down[:0:-1] + [first, second]


SIDE_ORDER = ((0, 1, 2, -1), (-2, -3, 3, 4))


def scatter_line(keep, send, down_type, few):
    other = to_sibling(send)
    half = CHIPS // 2
    up, down, own = begin(keep, other, few, down_type)
    for k in range(half - 1, 0, -1):
        up = onward(along_z(up, 1), keep, other, k, few)
        down = along_z(down, -1)
        if k > 1:
            share = keep[CHIPS - k + 1] + other[CHIPS - k + 1].astype(F32)
            down = (down.astype(F32) + share).astype(down_type)
    return own, along_z(up, 1), down


def narrow(out, value, few):
    if not few:
        out[...] = value.astype(BF)
        return
    span = value.shape[1] - 2 * few
    out[:, :span] = value[:, :span].astype(BF)
    whole = value[:, span : span + few] + value[:, span + few :]
    high = whole.astype(BF).astype(F32)
    out[:, span:] = jnp.concatenate([high, whole - high], axis=1).astype(BF)


def block(shape, k):
    return pl.BlockSpec((1, *shape), lambda _: (k, *[0] * len(shape)))


def begin(keep, other, few, down_type):
    shape = keep.shape[1:]
    half = CHIPS // 2

    def kernel(k0, k1, k2, o0, o1, o2, up, down, own):
        narrow(up, k0[0] + o0[0].astype(F32), few)
        down[...] = (k1[0] + o1[0].astype(F32)).astype(down_type)
        own[...] = k2[0] + o2[0].astype(F32)

    blocks = [block(shape, k) for k in (half, half + 1, 0)]
    return pl.pallas_call(
        kernel,
        grid=(1,),
        in_specs=blocks + blocks,
        out_specs=[pl.BlockSpec(shape, lambda _: (0,) * len(shape))] * 3,
        out_shape=[jax.ShapeDtypeStruct(shape, t) for t in (BF, down_type, F32)],
        name="begin",
    )(keep, keep, keep, other, other, other)


def onward(got, keep, other, k, few):
    shape = keep.shape[1:]
    plain = pl.BlockSpec(shape, lambda _: (0,) * len(shape))

    def kernel(g, k0, o0, out):
        narrow(out, g[...].astype(F32) + k0[0] + o0[0].astype(F32), few)

    return pl.pallas_call(
        kernel,
        grid=(1,),
        in_specs=[plain, block(shape, k), block(shape, k)],
        out_specs=plain,
        out_shape=jax.ShapeDtypeStruct(shape, BF),
        name="onward",
    )(got, keep, other)


def stack_kernel(*refs):
    out = refs[-1]
    for n, ref in enumerate(refs[:-1]):
        out[n] = ref[...]


def stack(*parts):
    return pl.pallas_call(
        stack_kernel,
        out_shape=jax.ShapeDtypeStruct((len(parts), *parts[0].shape), parts[0].dtype),
        name="stack",
    )(*parts)


def samples_kernel(own, up, down, target, wide, line):
    acc = own[...] + up[...].astype(F32) + down[...].astype(F32)
    span = target.shape[1]
    few = (acc.shape[1] - span) // 2
    wide[...] = acc[:, :span]
    line[:, :span] = acc[:, :span].astype(BF)
    line[:, span : 2 * span] = target[...]
    share = acc[:, span : span + few] + acc[:, span + few :]
    high = share.astype(BF).astype(F32)
    line[:, 2 * span :] = jnp.concatenate([high, share - high], axis=1).astype(BF)


def finish_kernel(own, up, down, out):
    order = out.shape[0] * CHIPS * CORES
    for i in range(own.shape[0]):
        acc = own[i] + up[i].astype(F32) + down[i].astype(F32)
        out[:, i, :] = acc * (1.0 / order)


def line_rows(q, k, sibling):
    core = q & 1
    chip = ((q >> 1) - k) & (CHIPS - 1)
    return chip * CORES + (core ^ sibling)


def forward_rows(q, k, sibling):
    core = q & 1
    chip = ((q >> 1) + k) & (CHIPS - 1)
    return chip * CORES + (core ^ sibling)


def put_line(q, k, sibling, piece, whole, target, share):
    few = piece.shape[1] // 17 // 2
    span = piece.shape[1] // 17 * 8
    place = line_rows(q, k, sibling)
    row = pl.multiple_of(place * span, span)
    whole[:, pl.ds(row, span), :] = piece[:, :span]
    target[:, pl.ds(row, span), :] = piece[:, span : 2 * span]
    parts = piece[:, 2 * span :].astype(F32)
    share[:, pl.ds(pl.multiple_of(place * few, few), few), :] = parts[:, :few] + parts[:, few:]


def place_plane(p, pieces, swap, whole, start, stop):
    span = pieces[0].shape[2]
    if len(pieces) == SIDE:
        parts = [(piece, d, 0) for d, piece in enumerate(pieces)]
    else:
        first, near, even, odd, far = pieces
        parts = [(first, 0, 0), (near, 1, 0), (even, 2, 0), (odd, 2, 1), (far, 3, 0)]
    for piece, d, low in parts:
        lo, hi = max(low, start), min(low + piece.shape[1], stop)
        if lo >= hi:
            continue
        for e in range(SIDE):
            dx, dy = (e, d) if swap else (d, e)
            x = ((p >> 2) - dx) & (SIDE - 1)
            y = ((p & 3) - dy) & (SIDE - 1)
            row = pl.multiple_of((x * SIDE + y) * span, span)
            whole[lo - start : hi - start, pl.ds(row, span), :] = piece[e, lo - low : hi - low]


def spread(q, i, source, keep, send, share=None):
    span = source.shape[0] // (CHIPS * CORES)
    for k in range(CHIPS):
        for sibling, out, kind in ((0, keep, F32), (1, send, BF)):
            place = forward_rows(q, k, sibling)
            row = pl.multiple_of(place * span, span)
            out[k, i, :span] = source[pl.ds(row, span), :].astype(kind)
            if share is not None:
                few = share.shape[0] // (CHIPS * CORES)
                part = share[pl.ds(pl.multiple_of(place * few, few), few), :]
                high = part if kind == F32 else part.astype(BF).astype(F32)
                out[k, i, span:] = jnp.concatenate([high, part - high], axis=0).astype(kind)


PIECES = SIDE + 1


def sample_kernel(tiles, columns):
    def kernel(p_ref, q_ref, ranks, left_hbm, right_hbm, tright, *refs):
        right_pieces, refs = refs[:SIDE], refs[SIDE:]
        left_pieces, refs = refs[:PIECES], refs[PIECES:]
        coupling, keep, send, lefts, pivot, probe, flip, ps, share, result, left, right, done = refs
        copies = [
            pltpu.make_async_copy(right_hbm, right, done.at[0]),
            pltpu.make_async_copy(left_hbm, left, done.at[1]),
        ]
        for copy in copies:
            copy.start()
        p, q = p_ref[0], q_ref[0]
        place_plane(p, left_pieces, True, lefts, 0, columns)
        place_plane(p, left_pieces, True, probe, columns, columns + 1)
        for j in range(columns):
            ps[j] = dims(lefts[j].T, probe[0], 1, 0)
        place_plane(p, right_pieces, False, pivot, 0, columns)
        for j in range(columns):
            flip[j] = pivot[j].T
        span = tright.shape[1]
        sketch = probe[0, pl.ds(pl.multiple_of(q * span, span), span), :]
        for copy in copies:
            copy.wait()

        def tile(i, carry):
            weights = []
            for j in range(columns):
                coup = dims(flip[j], right[i, j], 1, 0).T
                row = lax.broadcasted_iota(jnp.int32, coup.shape, 0)
                coup = jnp.where(row < ranks[i, j], coup, 0.0)
                coupling[i, j] = coup
                weights.append((-fine(coup, ps[j], 1, 0)).astype(BF))
            u = jnp.concatenate([left[i, j] for j in range(columns)], axis=1)
            share[...] = dims(tright[i], sketch, 0, 0)
            result[...] = dims(u, jnp.concatenate(weights, axis=0), 1, 0)
            spread(q, i, result, keep, send, share)
            return carry

        lax.fori_loop(0, tiles, tile, 0)

    return kernel


def eliminate(m, width):
    lane = lax.broadcasted_iota(jnp.int32, (8, width), 1)
    sub = lax.broadcasted_iota(jnp.int32, (8, width), 0)
    within = lane & (NB - 1)
    base = lane - within
    for k in range(0, NB, 2):
        b, r = k // 8, k % 8
        at0, at1 = within == k, within == k + 1
        g0 = [jnp.take_along_axis(m[n], base + k, axis=1) if n >= b else None for n in range(len(m))]
        g1 = [jnp.take_along_axis(m[n], base + (k + 1), axis=1) if n >= b else None for n in range(len(m))]
        row0, row1 = m[b][r : r + 1], m[b][r + 1 : r + 2]
        i0 = 1.0 / g0[b][r : r + 1]
        up, low = g1[b][r : r + 1], g0[b][r + 1 : r + 2]
        ratio = up * i0
        i1 = 1.0 / (g1[b][r + 1 : r + 2] - low * ratio)
        at0r, at1r = at0[:1], at1[:1]
        s0 = jnp.where(at0r, i0, row0 * i0)
        next_row = jnp.where(at0r, 0.0, row1) - low * s0
        s1 = jnp.where(at1r, i1, next_row * i1)
        s0 = jnp.where(at1r, 0.0, s0)
        for n in range(b, len(m)):
            new = jnp.where(at0 | at1, 0.0, m[n]) - g0[n] * s0 - (g1[n] - g0[n] * ratio) * s1
            if n == b:
                new = jnp.where(sub > r + 1, new, jnp.where(sub == r + 1, next_row, m[n]))
            m[n] = new
    return m


def factor_inverse(gram):
    tiles, rank, _ = gram.shape
    width = tiles * NB
    lane = lax.broadcasted_iota(jnp.int32, (NB, width), 1)
    row = lax.broadcasted_iota(jnp.int32, (NB, width), 0)
    within = lane & (NB - 1)
    square_row = lax.broadcasted_iota(jnp.int32, (width, width), 0)
    square_lane = lax.broadcasted_iota(jnp.int32, (width, width), 1)
    same = (square_row & -NB) == (square_lane & -NB)
    full_lane = lax.broadcasted_iota(jnp.int32, (rank, rank), 1)
    for start in range(0, rank, NB):
        stop = start + NB
        block = slice(start, stop)
        packed = jnp.concatenate([gram[i, block, block] for i in range(tiles)], axis=1)
        m = eliminate([packed[n : n + 8] for n in range(0, NB, 8)], width)
        m = jnp.concatenate(m, axis=0)
        pivots = jnp.take_along_axis(m, lane - within + row, axis=1)
        unit = jnp.where(within == row, 1.0, jnp.where(within < row, m, 0.0)) / jnp.sqrt(pivots)
        diagonal = jnp.where(same, jnp.concatenate([unit] * tiles, axis=0), 0.0)
        lines = fine(diagonal, jnp.concatenate([gram[i, block, :] for i in range(tiles)], axis=0), 1, 0)
        for i in range(tiles):
            line = lines[i * NB : (i + 1) * NB]
            own = pltpu.roll(unit, (start - i * NB) % width, 1) if (start - i * NB) % width else unit
            inside = (lane >= start) & (lane < stop)
            line = jnp.where(inside, own, line)
            gram[i, block, :] = jnp.where(lane < stop, line, 0.0)
            if stop < rank:
                update = fine(line, line, 0, 0)[stop:]
                rest = gram[i, stop:, :]
                zero = (full_lane[stop:] >= start) & (full_lane[stop:] < stop)
                gram[i, stop:, :] = jnp.where(zero, 0.0, rest) - update


def project_kernel(tiles, columns):
    def kernel(q_ref, left_hbm, coupling, tright, pivot, wide, *refs):
        line_pieces, refs = refs[:CHIPS], refs[CHIPS:]
        side_pieces, refs = refs[:2], refs[2:]
        exact, gram, keep, send, whole, target, share, flipped, result, left, done = refs
        copy = pltpu.make_async_copy(left_hbm, left, done)
        copy.start()
        q = q_ref[0]
        order = whole.shape[1]
        own = pl.ds(pl.multiple_of(q * wide.shape[1], wide.shape[1]), wide.shape[1])
        for k, piece in enumerate(line_pieces):
            put_line(q, k, 0, piece[...], whole, target, share)
        for piece, ks in zip(side_pieces, SIDE_ORDER):
            for n, k in enumerate(ks):
                put_line(q, k, 1, piece[n], whole, target, share)

        def square(i, carry):
            both = jnp.concatenate(halves(share[i]), axis=0)
            t = jnp.concatenate([target[i], target[i]], axis=1)
            term = dims(t, both, 1, 0)
            result[...] = term
            exact[i] = wide[i] + result[own, :]
            whole[i] = (whole[i].astype(F32) + term).astype(BF)
            flipped[i] = whole[i].T
            gram[i] = dims(flipped[i], whole[i], 1, 0) * (1.0 / order)
            return carry

        lax.fori_loop(0, tiles, square, 0)
        copy.wait()
        factor_inverse(gram)

        def tile(i, carry):
            inverse = gram[i]
            both = jnp.concatenate([left[i, j] for j in range(columns)], axis=1)
            seen = dims(flipped[i], both, 1, 0)
            span = inverse.shape[1]
            mixed = [
                fine(seen[:, j * span : (j + 1) * span], coupling[i, j], 1, 0) for j in range(columns)
            ]
            mixed.append(dims(flipped[i], target[i], 1, 0))
            solved = fine(inverse, jnp.concatenate(mixed, axis=1), 1, 0).astype(BF)
            u = jnp.concatenate([pivot[j] for j in range(columns)], axis=1)
            result[...] = -dims(u, solved[:, : columns * span], 1, 1)
            spread(q, i, result, keep, send)
            keep[0, i] = keep[0, i] + dims(tright[i], solved[:, columns * span :], 1, 1)
            return carry

        lax.fori_loop(0, tiles, tile, 0)

    return kernel


def vmem(n):
    return [pl.BlockSpec(memory_space=pltpu.VMEM)] * n


def basis_kernel(exact, inverse, out):
    for i in range(exact.shape[0]):
        out[:, i, :] = fine(exact[i], inverse[i], 1, 1)


def anywhere(n):
    return [pl.BlockSpec(memory_space=pl.ANY)] * n


def smem(n):
    return [pl.BlockSpec(memory_space=pltpu.SMEM)] * n


def per_device(
    left_factor, right_factor, pivot_left, pivot_right, target_left, target_right, probe, ranks
):
    tiles, columns, order, rank = left_factor.shape
    span = target_left.shape[0]
    n_col = CHIPS * CORES
    p = jnp.full((1,), lax.axis_index("prow"), jnp.int32)
    q = jnp.full((1,), lax.axis_index("pcol"), jnp.int32)
    right_first = first_stage(pivot_right, along_y)
    left_first = first_stage(jnp.concatenate([pivot_left, probe[None]]), along_x)
    right_plane = second_stage(right_first, along_x, "rights")
    left_plane = second_stage(left_first, along_y, "lefts")
    left_own = jnp.transpose(target_left, (1, 0, 2))
    right_own = jnp.transpose(target_right, (1, 0, 2))

    few = 2 * rank // n_col
    tall = (CHIPS, tiles, span + few, rank)
    coupling, keep, send, pivot = pl.pallas_call(
        sample_kernel(tiles, columns),
        out_shape=[
            jax.ShapeDtypeStruct((tiles, columns, rank, rank), F32),
            jax.ShapeDtypeStruct(tall, F32),
            jax.ShapeDtypeStruct(tall, BF),
            jax.ShapeDtypeStruct((columns, order, rank), BF),
        ],
        in_specs=smem(3) + anywhere(2) + vmem(1 + SIDE + PIECES),
        scratch_shapes=[
            pltpu.VMEM((columns, order, rank), BF),
            pltpu.VMEM((1, order, rank), BF),
            pltpu.VMEM((columns, rank, order), BF),
            pltpu.VMEM((columns, rank, rank), F32),
            pltpu.VMEM((rank, rank), F32),
            pltpu.VMEM((order, rank), F32),
            pltpu.VMEM(left_factor.shape, BF),
            pltpu.VMEM(left_factor.shape, BF),
            pltpu.SemaphoreType.DMA((2,)),
        ],
        name="sample",
    )(p, q, ranks, left_factor, right_factor, right_own, *right_plane, *left_plane)

    wide, line = pl.pallas_call(
        samples_kernel,
        out_shape=[
            jax.ShapeDtypeStruct((tiles, span, rank), F32),
            jax.ShapeDtypeStruct((tiles, 2 * span + few, rank), BF),
        ],
        name="samples_sum",
    )(*scatter_line(keep, send, F32, few // 2), left_own)

    share = (CHIPS, tiles, span, rank)
    exact, inverse, keep, send = pl.pallas_call(
        project_kernel(tiles, columns),
        out_shape=[
            jax.ShapeDtypeStruct((tiles, span, rank), F32),
            jax.ShapeDtypeStruct((tiles, rank, rank), F32),
            jax.ShapeDtypeStruct(share, F32),
            jax.ShapeDtypeStruct(share, BF),
        ],
        in_specs=smem(1) + anywhere(1) + vmem(4 + CHIPS + 2),
        scratch_shapes=[
            pltpu.VMEM((tiles, order, rank), BF),
            pltpu.VMEM((tiles, order, rank), BF),
            pltpu.VMEM((tiles, rank, rank), F32),
            pltpu.VMEM((tiles, rank, order), BF),
            pltpu.VMEM((order, rank), F32),
            pltpu.VMEM(left_factor.shape, BF),
            pltpu.SemaphoreType.DMA,
        ],
        name="project",
    )(q, left_factor, coupling, right_own, pivot, wide, *gather_line(line))
    basis = pl.pallas_call(
        basis_kernel, out_shape=jax.ShapeDtypeStruct((span, tiles, rank), F32), name="basis"
    )(exact, inverse)
    coefficient = pl.pallas_call(
        finish_kernel,
        out_shape=jax.ShapeDtypeStruct((span, tiles, rank), F32),
        name="finish",
    )(*scatter_line(keep, send, BF, 0))
    return (basis, coefficient)


def solution(mesh):
    in_specs = (
        P("prow", "pcol", None, None),
        P("prow", "pcol", None, None),
        P("pcol", "prow", None),
        P("pcol", "prow", None),
        P("pcol", "prow", None),
        P("pcol", "prow", None),
        P("prow", None),
        P("prow", "pcol"),
    )
    out_specs = (P("pcol", "prow", None), P("pcol", "prow", None))

    return jax.shard_map(per_device, mesh=mesh, in_specs=in_specs, out_specs=out_specs, check_vma=False)
```

profile of v0, /device:TPU:6, one launch (start us, length us, event | category | flops | bytes accessed | tf_op | source)
XLA Modules:
  0.0 218.6 jit_solution(15975182817612367035)
XLA Ops:
  3.1 2.1 collective-permute-start.6
  5.2 3.3 %collective-permute-done.7 = bf16[3,128,128]{2,1,0:T(8,128)(2,1)S(1)} collective-permute-done((bf16[3,128,128]{2,1,0:T(8,128)(2,1)S(1)}, bf16[3,128,128]{2,1,0:T(8,128)(2,1)S(1)}, u32[]{:S(2)}, u32[]{:S(2)}) %collective-permute-start.7) | collective-permute-done | bytes 98336 | tf_op jit(solution)/shard_map/ppermute | solution.py:50
  8.5 2.5 %collective-permute-done.8 = bf16[3,128,128]{2,1,0:T(8,128)(2,1)S(1)} collective-permute-done((bf16[3,128,128]{2,1,0:T(8,128)(2,1)S(1)}, bf16[3,128,128]{2,1,0:T(8,128)(2,1)S(1)}, u32[]{:S(2)}, u32[]{:S(2)}) %collective-permute-start.8) | collective-permute-done | bytes 98336 | tf_op jit(solution)/shard_map/ppermute | solution.py:50
  11.0 3.1 %collective-permute-start.11 = (bf16[4,3,128,128]{3,2,1,0:T(8,128)(2,1)S(1)}, bf16[4,3,128,128]{3,2,1,0:T(8,128)(2,1)S(1)}, u32[]{:S(2)}, u32[]{:S(2)}) collective-permute-start(bf16[4,3,128,128]{3,2,1,0:T(8,128)(2,1)S(1)} %pad_maximum_fusion.refs_4_), channel_id=1, source_target_pairs={{0,48},{16,0},{32,16},{48,32},{64,112},{80,64},{96,80},{112,96},{1... | collective-permute-start | bytes 1179656 | tf_op jit(solution)/shard_map/ppermute | solution.py:44
  14.1 3.2 %collective-permute-start.2 = (bf16[2,128,128]{2,1,0:T(8,128)(2,1)}, bf16[2,128,128]{2,1,0:T(8,128)(2,1)S(1)}, u32[]{:S(2)}, u32[]{:S(2)}) collective-permute-start(bf16[2,128,128]{2,1,0:T(8,128)(2,1)} %param.11), channel_id=1, source_target_pairs={{0,48},{16,0},{32,16},{48,32},{64,112},{80,64},{96,80},{112,96},{1... | collective-permute-start | bytes 196616 | tf_op jit(solution)/shard_map/ppermute | solution.py:44
  18.3 2.9 %collective-permute-done = bf16[2,128,128]{2,1,0:T(8,128)(2,1)S(1)} collective-permute-done((bf16[2,128,128]{2,1,0:T(8,128)(2,1)}, bf16[2,128,128]{2,1,0:T(8,128)(2,1)S(1)}, u32[]{:S(2)}, u32[]{:S(2)}) %collective-permute-start) | collective-permute-done | bytes 65568 | tf_op jit(solution)/shard_map/ppermute | solution.py:44
  21.2 5.4 %collective-permute-done.2 = bf16[2,128,128]{2,1,0:T(8,128)(2,1)S(1)} collective-permute-done((bf16[2,128,128]{2,1,0:T(8,128)(2,1)}, bf16[2,128,128]{2,1,0:T(8,128)(2,1)S(1)}, u32[]{:S(2)}, u32[]{:S(2)}) %collective-permute-start.2) | collective-permute-done | bytes 65568 | tf_op jit(solution)/shard_map/ppermute | solution.py:44
  27.6 2.1 collective-permute-start.4
  29.7 2.5 %collective-permute-start.3 = (bf16[4,2,128,128]{3,2,1,0:T(8,128)(2,1)S(1)}, bf16[4,2,128,128]{3,2,1,0:T(8,128)(2,1)S(1)}, u32[]{:S(2)}, u32[]{:S(2)}) collective-permute-start(bf16[4,2,128,128]{3,2,1,0:T(8,128)(2,1)S(1)} %pad_maximum_fusion.1.refs_0_), channel_id=1, source_target_pairs={{0,64},{16,80},{32,96},{48,112},{64,128},{80,144},{96,160},{112,17... | collective-permute-start | bytes 786440 | tf_op jit(solution)/shard_map/ppermute | solution.py:50
  32.3 3.7 %collective-permute-start.12 = (bf16[4,2,128,128]{3,2,1,0:T(8,128)(2,1)S(1)}, bf16[4,2,128,128]{3,2,1,0:T(8,128)(2,1)S(1)}, u32[]{:S(2)}, u32[]{:S(2)}) collective-permute-start(bf16[4,2,128,128]{3,2,1,0:T(8,128)(2,1)S(1)} %slice.41), channel_id=1, source_target_pairs={{0,48},{16,0},{32,16},{48,32},{64,112},{80,64},{96,80},{112,96},{1... | collective-permute-start | bytes 786440 | tf_op jit(solution)/shard_map/ppermute | solution.py:44
  37.3 3.5 %collective-permute-done.5.refs_3_ = bf16[4,2,128,128]{3,2,1,0:T(8,128)(2,1)S(1)} collective-permute-done((bf16[4,2,128,128]{3,2,1,0:T(8,128)(2,1)S(1)}, bf16[4,2,128,128]{3,2,1,0:T(8,128)(2,1)S(1)}, u32[]{:S(2)}, u32[]{:S(2)}) %collective-permute-start.5) | collective-permute-done | bytes 262176 | tf_op jit(solution)/shard_map/ppermute | solution.py:50
  42.0 13.0 %sample.1 = (f32[4,2,128,128]{3,2,1,0:T(8,128)}, f32[8,4,144,128]{3,2,1,0:T(8,128)}, bf16[8,4,144,128]{3,2,1,0:T(8,128)(2,1)}, bf16[2,2048,128]{2,1,0:T(8,128)(2,1)}) custom-call(s32[1]{0:T(128)} %bitcast.1.p_ref, s32[1]{0:T(128)} %bitcast.q_ref, s32[4,2]{1,0:T(4,128)} %copy.11.ranks, bf16[4,2,2048,128]{3,2,1,0:T(8,128)(2,1)} %left_hbm.3, ...), custom_call_target="tpu_custom_call" | custom-call | tf_op jit(solution)/shard_map/sample/pallas_call | solution.py:431
  55.1 3.0 %collective-permute-done.13.o0.o1.o2 = bf16[8,4,144,128]{3,2,1,0:T(8,128)(2,1)S(1)} collective-permute-done((bf16[8,4,144,128]{3,2,1,0:T(8,128)(2,1)}, bf16[8,4,144,128]{3,2,1,0:T(8,128)(2,1)S(1)}, u32[]{:S(2)}, u32[]{:S(2)}) %collective-permute-start.13) | collective-permute-done | bytes 1179680 | tf_op jit(solution)/shard_map/ppermute | solution.py:35
  59.1 2.2 %begin.2 = (bf16[4,144,128]{2,1,0:T(8,128)(2,1)}, f32[4,144,128]{2,1,0:T(8,128)}, f32[4,144,128]{2,1,0:T(8,128)}) custom-call(f32[8,4,144,128]{3,2,1,0:T(8,128)} %get-tuple-element.20.k0.k1.k2, f32[8,4,144,128]{3,2,1,0:T(8,128)} %get-tuple-element.20.k0.k1.k2, f32[8,4,144,128]{3,2,1,0:T(8,128)} %get-tuple-element.20.k0.k1.k2, ...), custom_call_target="tpu_custom_call" | custom-call | tf_op jit(solution)/shard_map/begin/pallas_call | solution.py:122
  61.3 5.9 %collective-permute-start.18 = (f32[4,144,128]{2,1,0:T(8,128)}, f32[4,144,128]{2,1,0:T(8,128)S(1)}, u32[]{:S(2)}, u32[]{:S(2)}) collective-permute-start(f32[4,144,128]{2,1,0:T(8,128)} %get-tuple-element.24), channel_id=1, source_target_pairs={{0,14},{1,15},{2,0},{3,1},{4,2},{5,3},{6,4},{7,5},{8,6},{9,7},{10,... | collective-permute-start | bytes 884744 | tf_op jit(solution)/shard_map/ppermute | solution.py:40
  67.2 6.9 %collective-permute-done.18 = f32[4,144,128]{2,1,0:T(8,128)S(1)} collective-permute-done((f32[4,144,128]{2,1,0:T(8,128)}, f32[4,144,128]{2,1,0:T(8,128)S(1)}, u32[]{:S(2)}, u32[]{:S(2)}) %collective-permute-start.18) | collective-permute-done | bytes 294944 | tf_op jit(solution)/shard_map/ppermute | solution.py:40
  75.1 3.7 %collective-permute-start.19 = (f32[4,144,128]{2,1,0:T(8,128)S(1)}, f32[4,144,128]{2,1,0:T(8,128)S(1)}, u32[]{:S(2)}, u32[]{:S(2)}) collective-permute-start(f32[4,144,128]{2,1,0:T(8,128)S(1)} %bitcast_add_fusion.1), channel_id=1, source_target_pairs={{0,14},{1,15},{2,0},{3,1},{4,2},{5,3},{6,4},{7,5},{8,6},{9,7},{10,... | collective-permute-start | bytes 884744 | tf_op jit(solution)/shard_map/ppermute | solution.py:40
  79.4 1.8 onward.6
  81.2 6.6 %collective-permute-done.15.g = bf16[4,144,128]{2,1,0:T(8,128)(2,1)S(1)} collective-permute-done((bf16[4,144,128]{2,1,0:T(8,128)(2,1)}, bf16[4,144,128]{2,1,0:T(8,128)(2,1)S(1)}, u32[]{:S(2)}, u32[]{:S(2)}) %collective-permute-start.15) | collective-permute-done | bytes 147488 | tf_op jit(solution)/shard_map/ppermute | solution.py:40
  88.4 1.8 onward.7
  91.3 3.3 %collective-permute-start.20 = (f32[4,144,128]{2,1,0:T(8,128)S(1)}, f32[4,144,128]{2,1,0:T(8,128)S(1)}, u32[]{:S(2)}, u32[]{:S(2)}) collective-permute-start(f32[4,144,128]{2,1,0:T(8,128)S(1)} %bitcast_add_fusion), channel_id=1, source_target_pairs={{0,14},{1,15},{2,0},{3,1},{4,2},{5,3},{6,4},{7,5},{8,6},{9,7},{10,... | collective-permute-start | bytes 884744 | tf_op jit(solution)/shard_map/ppermute | solution.py:40
  94.6 2.2 %collective-permute-done.16.g = bf16[4,144,128]{2,1,0:T(8,128)(2,1)S(1)} collective-permute-done((bf16[4,144,128]{2,1,0:T(8,128)(2,1)}, bf16[4,144,128]{2,1,0:T(8,128)(2,1)S(1)}, u32[]{:S(2)}, u32[]{:S(2)}) %collective-permute-start.16) | collective-permute-done | bytes 147488 | tf_op jit(solution)/shard_map/ppermute | solution.py:40
  97.4 1.8 onward.8
  99.9 5.9 %collective-permute-done.17.up = bf16[4,144,128]{2,1,0:T(8,128)(2,1)S(1)} collective-permute-done((bf16[4,144,128]{2,1,0:T(8,128)(2,1)}, bf16[4,144,128]{2,1,0:T(8,128)(2,1)S(1)}, u32[]{:S(2)}, u32[]{:S(2)}) %collective-permute-start.17) | collective-permute-done | bytes 147488 | tf_op jit(solution)/shard_map/ppermute | solution.py:40
  106.6 2.0 samples_sum.1
  108.6 3.2 %collective-permute-start.25 = (bf16[4,272,128]{2,1,0:T(8,128)(2,1)}, bf16[4,272,128]{2,1,0:T(8,128)(2,1)S(1)}, u32[]{:S(2)}, u32[]{:S(2)}) collective-permute-start(bf16[4,272,128]{2,1,0:T(8,128)(2,1)} %get-tuple-element.26.refs_0_), channel_id=1, source_target_pairs={{0,14},{1,15},{2,0},{3,1},{4,2},{5,3},{6,4},{7,5},{8,6},{9,7},{10,... | collective-permute-start | bytes 835592 | tf_op jit(solution)/shard_map/ppermute | solution.py:40
  111.8 6.5 %collective-permute-done.21.refs_1_ = bf16[4,272,128]{2,1,0:T(8,128)(2,1)S(1)} collective-permute-done((bf16[4,272,128]{2,1,0:T(8,128)(2,1)}, bf16[4,272,128]{2,1,0:T(8,128)(2,1)S(1)}, u32[]{:S(2)}, u32[]{:S(2)}) %collective-permute-start.21) | collective-permute-done | bytes 278560 | tf_op jit(solution)/shard_map/ppermute | solution.py:40
  118.4 3.5 %collective-permute-start.26 = (bf16[4,272,128]{2,1,0:T(8,128)(2,1)S(1)}, bf16[4,272,128]{2,1,0:T(8,128)(2,1)S(1)}, u32[]{:S(2)}, u32[]{:S(2)}) collective-permute-start(bf16[4,272,128]{2,1,0:T(8,128)(2,1)S(1)} %collective-permute-done.25.refs_3_.refs_7_), channel_id=1, source_target_pairs={{0,14},{1,15},{2,0},{3,1},{4,2},{5,3},{6,4},{7,5},{8,6},{9,7},{10,... | collective-permute-start | bytes 835592 | tf_op jit(solution)/shard_map/ppermute | solution.py:40
  121.9 7.2 %collective-permute-done.22.refs_2_ = bf16[4,272,128]{2,1,0:T(8,128)(2,1)S(1)} collective-permute-done((bf16[4,272,128]{2,1,0:T(8,128)(2,1)S(1)}, bf16[4,272,128]{2,1,0:T(8,128)(2,1)S(1)}, u32[]{:S(2)}, u32[]{:S(2)}) %collective-permute-start.22) | collective-permute-done | bytes 278560 | tf_op jit(solution)/shard_map/ppermute | solution.py:40
  129.1 3.3 %collective-permute-start.27 = (bf16[4,272,128]{2,1,0:T(8,128)(2,1)S(1)}, bf16[4,272,128]{2,1,0:T(8,128)(2,1)S(1)}, u32[]{:S(2)}, u32[]{:S(2)}) collective-permute-start(bf16[4,272,128]{2,1,0:T(8,128)(2,1)S(1)} %collective-permute-done.26.refs_0_.refs_6_), channel_id=1, source_target_pairs={{0,14},{1,15},{2,0},{3,1},{4,2},{5,3},{6,4},{7,5},{8,6},{9,7},{10,... | collective-permute-start | bytes 835592 | tf_op jit(solution)/shard_map/ppermute | solution.py:40
  132.4 6.6 %collective-permute-done.23.refs_2_.refs_3_ = bf16[4,272,128]{2,1,0:T(8,128)(2,1)S(1)} collective-permute-done((bf16[4,272,128]{2,1,0:T(8,128)(2,1)S(1)}, bf16[4,272,128]{2,1,0:T(8,128)(2,1)S(1)}, u32[]{:S(2)}, u32[]{:S(2)}) %collective-permute-start.23) | collective-permute-done | bytes 278560 | tf_op jit(solution)/shard_map/ppermute | solution.py:40
  139.0 2.4 %stack.42 = bf16[4,4,272,128]{3,2,1,0:T(8,128)(2,1)} custom-call(bf16[4,272,128]{2,1,0:T(8,128)(2,1)} %get-tuple-element.26.refs_0_, bf16[4,272,128]{2,1,0:T(8,128)(2,1)} %copy-done.3, bf16[4,272,128]{2,1,0:T(8,128)(2,1)} %copy-done.5, bf16[4,272,128]{2,1,0:T(8,128)(2,1)} %copy-done.4), custom_call_target="tpu_custom_call" | custom-call | tf_op jit(solution)/shard_map/stack/pallas_call | solution.py:156
  141.4 5.3 %collective-permute-done.24.refs_3_.refs_4_ = bf16[4,272,128]{2,1,0:T(8,128)(2,1)S(1)} collective-permute-done((bf16[4,272,128]{2,1,0:T(8,128)(2,1)S(1)}, bf16[4,272,128]{2,1,0:T(8,128)(2,1)S(1)}, u32[]{:S(2)}, u32[]{:S(2)}) %collective-permute-start.24) | collective-permute-done | bytes 278560 | tf_op jit(solution)/shard_map/ppermute | solution.py:40
  147.4 2.3 %stack.43 = bf16[4,4,272,128]{3,2,1,0:T(8,128)(2,1)} custom-call(bf16[4,272,128]{2,1,0:T(8,128)(2,1)} %copy-done.6, bf16[4,272,128]{2,1,0:T(8,128)(2,1)} %copy-done.8, bf16[4,272,128]{2,1,0:T(8,128)(2,1)} %copy-done.7, bf16[4,272,128]{2,1,0:T(8,128)(2,1)} %copy-done.9), custom_call_target="tpu_custom_call" | custom-call | tf_op jit(solution)/shard_map/stack/pallas_call | solution.py:156
  149.7 2.9 %collective-permute-done.29.refs_9_ = bf16[4,4,272,128]{3,2,1,0:T(8,128)(2,1)S(1)} collective-permute-done((bf16[4,4,272,128]{3,2,1,0:T(8,128)(2,1)}, bf16[4,4,272,128]{3,2,1,0:T(8,128)(2,1)S(1)}, u32[]{:S(2)}, u32[]{:S(2)}) %collective-permute-start.29) | collective-permute-done | bytes 1114144 | tf_op jit(solution)/shard_map/ppermute | solution.py:35
  153.7 23.0 %project.1 = (f32[4,128,128]{2,1,0:T(8,128)}, f32[4,128,128]{2,1,0:T(8,128)}, f32[8,4,128,128]{3,2,1,0:T(8,128)}, bf16[8,4,128,128]{3,2,1,0:T(8,128)(2,1)}) custom-call(s32[1]{0:T(128)} %bitcast.q_ref, bf16[4,2,2048,128]{3,2,1,0:T(8,128)(2,1)} %left_hbm.3, f32[4,2,128,128]{3,2,1,0:T(8,128)} %get-tuple-element.18.coupling, bf16[4,128,128]{2,1,0:T(8,128)(2,1)} %bitcast.31, ...), custom_call_target="tpu_custom_call" | custom-call | tf_op jit(solution)/shard_map/project/pallas_call | solution.py:464
  176.9 2.8 %collective-permute-done.30.o0.o1.o2 = bf16[8,4,128,128]{3,2,1,0:T(8,128)(2,1)S(1)} collective-permute-done((bf16[8,4,128,128]{3,2,1,0:T(8,128)(2,1)}, bf16[8,4,128,128]{3,2,1,0:T(8,128)(2,1)S(1)}, u32[]{:S(2)}, u32[]{:S(2)}) %collective-permute-start.30) | collective-permute-done | bytes 1048608 | tf_op jit(solution)/shard_map/ppermute | solution.py:35
  180.7 2.1 begin.3
  182.7 3.2 %collective-permute-start.35 = (bf16[4,128,128]{2,1,0:T(8,128)(2,1)}, bf16[4,128,128]{2,1,0:T(8,128)(2,1)S(1)}, u32[]{:S(2)}, u32[]{:S(2)}) collective-permute-start(bf16[4,128,128]{2,1,0:T(8,128)(2,1)} %get-tuple-element.33), channel_id=1, source_target_pairs={{0,14},{1,15},{2,0},{3,1},{4,2},{5,3},{6,4},{7,5},{8,6},{9,7},{10,... | collective-permute-start | bytes 393224 | tf_op jit(solution)/shard_map/ppermute | solution.py:40
  186.0 3.7 %collective-permute-done.31.g = bf16[4,128,128]{2,1,0:T(8,128)(2,1)S(1)} collective-permute-done((bf16[4,128,128]{2,1,0:T(8,128)(2,1)}, bf16[4,128,128]{2,1,0:T(8,128)(2,1)S(1)}, u32[]{:S(2)}, u32[]{:S(2)}) %collective-permute-start.31) | collective-permute-done | bytes 131104 | tf_op jit(solution)/shard_map/ppermute | solution.py:40
  193.1 3.3 %collective-permute-start.36 = (bf16[4,128,128]{2,1,0:T(8,128)(2,1)S(1)}, bf16[4,128,128]{2,1,0:T(8,128)(2,1)S(1)}, u32[]{:S(2)}, u32[]{:S(2)}) collective-permute-start(bf16[4,128,128]{2,1,0:T(8,128)(2,1)S(1)} %fusion.1), channel_id=1, source_target_pairs={{0,14},{1,15},{2,0},{3,1},{4,2},{5,3},{6,4},{7,5},{8,6},{9,7},{10,... | collective-permute-start | bytes 393224 | tf_op jit(solution)/shard_map/ppermute | solution.py:40
  196.4 2.0 collective-permute-done.32.g
  199.1 1.7 onward.10
  201.9 3.3 %collective-permute-start.37 = (bf16[4,128,128]{2,1,0:T(8,128)(2,1)S(1)}, bf16[4,128,128]{2,1,0:T(8,128)(2,1)S(1)}, u32[]{:S(2)}, u32[]{:S(2)}) collective-permute-start(bf16[4,128,128]{2,1,0:T(8,128)(2,1)S(1)} %fusion), channel_id=1, source_target_pairs={{0,14},{1,15},{2,0},{3,1},{4,2},{5,3},{6,4},{7,5},{8,6},{9,7},{10,... | collective-permute-start | bytes 393224 | tf_op jit(solution)/shard_map/ppermute | solution.py:40
  205.2 2.0 collective-permute-done.33.g
  209.7 2.2 basis.1
  211.8 4.2 %collective-permute-done.34.up = bf16[4,128,128]{2,1,0:T(8,128)(2,1)S(1)} collective-permute-done((bf16[4,128,128]{2,1,0:T(8,128)(2,1)}, bf16[4,128,128]{2,1,0:T(8,128)(2,1)S(1)}, u32[]{:S(2)}, u32[]{:S(2)}) %collective-permute-start.34) | collective-permute-done | bytes 131104 | tf_op jit(solution)/shard_map/ppermute | solution.py:40
  216.7 1.9 finish.1
  (121 shorter events, 24.6 us)
Async XLA Ops:
  0.6 35.3 %copy-start.32 = (s32[4,2]{0,1:T(2,128)S(1)}, s32[4,2]{0,1:T(2,128)}, u32[]{:S(2)}) copy-start(s32[4,2]{0,1:T(2,128)} %param.15) | copy-start | bytes 100
  0.6 36.0 %copy-start.25 = (bf16[128,4,128]{2,1,0:T(4,128)(2,1)S(1)}, bf16[128,4,128]{2,1,0:T(4,128)(2,1)}, u32[]{:S(2)}) copy-start(bf16[128,4,128]{2,1,0:T(4,128)(2,1)} %param.13) | copy-start | bytes 393220
  1.6 6.9 %collective-permute-start.7 = (bf16[3,128,128]{2,1,0:T(8,128)(2,1)S(1)}, bf16[3,128,128]{2,1,0:T(8,128)(2,1)S(1)}, u32[]{:S(2)}, u32[]{:S(2)}) collective-permute-start(bf16[3,128,128]{2,1,0:T(8,128)(2,1)S(1)} %get-tuple-element.35), channel_id=1, source_target_pairs={{0,128},{16,144},{32,160},{48,176},{64,192},{80,208},{96,224},{112... | collective-permute-start | bytes 294920 | tf_op jit(solution)/shard_map/ppermute | solution.py:50
  3.1 5.4 %collective-permute-start.6 = (bf16[3,128,128]{2,1,0:T(8,128)(2,1)S(1)}, bf16[3,128,128]{2,1,0:T(8,128)(2,1)S(1)}, u32[]{:S(2)}, u32[]{:S(2)}) collective-permute-start(bf16[3,128,128]{2,1,0:T(8,128)(2,1)S(1)} %get-tuple-element.35), channel_id=1, source_target_pairs={{0,64},{16,80},{32,96},{48,112},{64,128},{80,144},{96,160},{112,17... | collective-permute-start | bytes 294920 | tf_op jit(solution)/shard_map/ppermute | solution.py:50
  5.2 5.8 %collective-permute-start.8 = (bf16[3,128,128]{2,1,0:T(8,128)(2,1)S(1)}, bf16[3,128,128]{2,1,0:T(8,128)(2,1)S(1)}, u32[]{:S(2)}, u32[]{:S(2)}) collective-permute-start(bf16[3,128,128]{2,1,0:T(8,128)(2,1)S(1)} %get-tuple-element.35), channel_id=1, source_target_pairs={{0,192},{16,208},{32,224},{48,240},{64,0},{80,16},{96,32},{112,48}... | collective-permute-start | bytes 294920 | tf_op jit(solution)/shard_map/ppermute | solution.py:50
  11.0 29.9 %copy-start.2 = (bf16[4,3,128,128]{3,2,1,0:T(8,128)(2,1)}, bf16[4,3,128,128]{3,2,1,0:T(8,128)(2,1)S(1)}, u32[]{:S(2)}) copy-start(bf16[4,3,128,128]{3,2,1,0:T(8,128)(2,1)S(1)} %pad_maximum_fusion.refs_4_) | copy-start | bytes 1179652
  11.0 18.7 %collective-permute-start.11 = (bf16[4,3,128,128]{3,2,1,0:T(8,128)(2,1)S(1)}, bf16[4,3,128,128]{3,2,1,0:T(8,128)(2,1)S(1)}, u32[]{:S(2)}, u32[]{:S(2)}) collective-permute-start(bf16[4,3,128,128]{3,2,1,0:T(8,128)(2,1)S(1)} %pad_maximum_fusion.refs_4_), channel_id=1, source_target_pairs={{0,48},{16,0},{32,16},{48,32},{64,112},{80,64},{96,80},{112,96},{1... | collective-permute-start | bytes 1179656 | tf_op jit(solution)/shard_map/ppermute | solution.py:44
  14.1 7.1 %collective-permute-start = (bf16[2,128,128]{2,1,0:T(8,128)(2,1)}, bf16[2,128,128]{2,1,0:T(8,128)(2,1)S(1)}, u32[]{:S(2)}, u32[]{:S(2)}) collective-permute-start(bf16[2,128,128]{2,1,0:T(8,128)(2,1)} %param.11), channel_id=1, source_target_pairs={{0,16},{16,32},{32,48},{48,0},{64,80},{80,96},{96,112},{112,64},{1... | collective-permute-start | bytes 196616 | tf_op jit(solution)/shard_map/ppermute | solution.py:44
  14.1 12.5 %collective-permute-start.2 = (bf16[2,128,128]{2,1,0:T(8,128)(2,1)}, bf16[2,128,128]{2,1,0:T(8,128)(2,1)S(1)}, u32[]{:S(2)}, u32[]{:S(2)}) collective-permute-start(bf16[2,128,128]{2,1,0:T(8,128)(2,1)} %param.11), channel_id=1, source_target_pairs={{0,48},{16,0},{32,16},{48,32},{64,112},{80,64},{96,80},{112,96},{1... | collective-permute-start | bytes 196616 | tf_op jit(solution)/shard_map/ppermute | solution.py:44
  17.4 9.3 %collective-permute-start.1 = (bf16[2,128,128]{2,1,0:T(8,128)(2,1)}, bf16[2,128,128]{2,1,0:T(8,128)(2,1)S(1)}, u32[]{:S(2)}, u32[]{:S(2)}) collective-permute-start(bf16[2,128,128]{2,1,0:T(8,128)(2,1)} %param.11), channel_id=1, source_target_pairs={{0,32},{16,48},{32,0},{48,16},{64,96},{80,112},{96,64},{112,80},{1... | collective-permute-start | bytes 196616 | tf_op jit(solution)/shard_map/ppermute | solution.py:44
  17.4 23.5 %collective-permute-start.9 = (bf16[4,3,128,128]{3,2,1,0:T(8,128)(2,1)S(1)}, bf16[4,3,128,128]{3,2,1,0:T(8,128)(2,1)S(1)}, u32[]{:S(2)}, u32[]{:S(2)}) collective-permute-start(bf16[4,3,128,128]{3,2,1,0:T(8,128)(2,1)S(1)} %pad_maximum_fusion.refs_4_), channel_id=1, source_target_pairs={{0,16},{16,32},{32,48},{48,0},{64,80},{80,96},{96,112},{112,64},{1... | collective-permute-start | bytes 1179656 | tf_op jit(solution)/shard_map/ppermute | solution.py:44
  21.2 11.1 %collective-permute-start.10 = (bf16[4,1,128,128]{3,2,1,0:T(8,128)(2,1)S(1)}, bf16[4,1,128,128]{3,2,1,0:T(8,128)(2,1)S(1)}, u32[]{:S(2)}, u32[]{:S(2)}) collective-permute-start(bf16[4,1,128,128]{3,2,1,0:T(8,128)(2,1)S(1)} %slice.40), channel_id=1, source_target_pairs={{0,32},{16,48},{32,0},{48,16},{64,96},{80,112},{96,64},{112,80},{1... | collective-permute-start | bytes 393224 | tf_op jit(solution)/shard_map/ppermute | solution.py:44
  27.5 13.4 %copy-start.13 = (bf16[4,2,128,128]{3,2,1,0:T(8,128)(2,1)}, bf16[4,2,128,128]{3,2,1,0:T(8,128)(2,1)S(1)}, u32[]{:S(2)}) copy-start(bf16[4,2,128,128]{3,2,1,0:T(8,128)(2,1)S(1)} %pad_maximum_fusion.1.refs_0_) | copy-start | bytes 786436
  27.6 13.3 %collective-permute-start.5 = (bf16[4,2,128,128]{3,2,1,0:T(8,128)(2,1)S(1)}, bf16[4,2,128,128]{3,2,1,0:T(8,128)(2,1)S(1)}, u32[]{:S(2)}, u32[]{:S(2)}) collective-permute-start(bf16[4,2,128,128]{3,2,1,0:T(8,128)(2,1)S(1)} %pad_maximum_fusion.1.refs_0_), channel_id=1, source_target_pairs={{0,192},{16,208},{32,224},{48,240},{64,0},{80,16},{96,32},{112,48}... | collective-permute-start | bytes 786440 | tf_op jit(solution)/shard_map/ppermute | solution.py:50
  27.6 13.2 %collective-permute-start.4 = (bf16[4,2,128,128]{3,2,1,0:T(8,128)(2,1)S(1)}, bf16[4,2,128,128]{3,2,1,0:T(8,128)(2,1)S(1)}, u32[]{:S(2)}, u32[]{:S(2)}) collective-permute-start(bf16[4,2,128,128]{3,2,1,0:T(8,128)(2,1)S(1)} %pad_maximum_fusion.1.refs_0_), channel_id=1, source_target_pairs={{0,128},{16,144},{32,160},{48,176},{64,192},{80,208},{96,224},{112... | collective-permute-start | bytes 786440 | tf_op jit(solution)/shard_map/ppermute | solution.py:50
  29.7 11.2 %copy-start.12 = (bf16[4,3,128,128]{3,2,1,0:T(8,128)(2,1)}, bf16[4,3,128,128]{3,2,1,0:T(8,128)(2,1)S(1)}, u32[]{:S(2)}) copy-start(bf16[4,3,128,128]{3,2,1,0:T(8,128)(2,1)S(1)} %collective-permute-done.11.refs_8_) | copy-start | bytes 1179652
  29.7 11.1 %collective-permute-start.3 = (bf16[4,2,128,128]{3,2,1,0:T(8,128)(2,1)S(1)}, bf16[4,2,128,128]{3,2,1,0:T(8,128)(2,1)S(1)}, u32[]{:S(2)}, u32[]{:S(2)}) collective-permute-start(bf16[4,2,128,128]{3,2,1,0:T(8,128)(2,1)S(1)} %pad_maximum_fusion.1.refs_0_), channel_id=1, source_target_pairs={{0,64},{16,80},{32,96},{48,112},{64,128},{80,144},{96,160},{112,17... | collective-permute-start | bytes 786440 | tf_op jit(solution)/shard_map/ppermute | solution.py:50
  32.3 8.6 %copy-start.24 = (bf16[4,1,128,128]{3,2,1,0:T(8,128)(2,1)}, bf16[4,1,128,128]{3,2,1,0:T(8,128)(2,1)S(1)}, u32[]{:S(2)}) copy-start(bf16[4,1,128,128]{3,2,1,0:T(8,128)(2,1)S(1)} %collective-permute-done.10.refs_6_) | copy-start | bytes 393220
  32.3 8.6 %collective-permute-start.12 = (bf16[4,2,128,128]{3,2,1,0:T(8,128)(2,1)S(1)}, bf16[4,2,128,128]{3,2,1,0:T(8,128)(2,1)S(1)}, u32[]{:S(2)}, u32[]{:S(2)}) collective-permute-start(bf16[4,2,128,128]{3,2,1,0:T(8,128)(2,1)S(1)} %slice.41), channel_id=1, source_target_pairs={{0,48},{16,0},{32,16},{48,32},{64,112},{80,64},{96,80},{112,96},{1... | collective-permute-start | bytes 786440 | tf_op jit(solution)/shard_map/ppermute | solution.py:44
  55.0 3.1 %collective-permute-start.13 = (bf16[8,4,144,128]{3,2,1,0:T(8,128)(2,1)}, bf16[8,4,144,128]{3,2,1,0:T(8,128)(2,1)S(1)}, u32[]{:S(2)}, u32[]{:S(2)}) collective-permute-start(bf16[8,4,144,128]{3,2,1,0:T(8,128)(2,1)} %get-tuple-element.21), channel_id=1, source_target_pairs={{0,1},{1,0},{2,3},{3,2},{4,5},{5,4},{6,7},{7,6},{8,9},{9,8},{10,11... | collective-permute-start | bytes 3538952 | tf_op jit(solution)/shard_map/ppermute | solution.py:35
  61.3 12.7 %collective-permute-start.18 = (f32[4,144,128]{2,1,0:T(8,128)}, f32[4,144,128]{2,1,0:T(8,128)S(1)}, u32[]{:S(2)}, u32[]{:S(2)}) collective-permute-start(f32[4,144,128]{2,1,0:T(8,128)} %get-tuple-element.24), channel_id=1, source_target_pairs={{0,14},{1,15},{2,0},{3,1},{4,2},{5,3},{6,4},{7,5},{8,6},{9,7},{10,... | collective-permute-start | bytes 884744 | tf_op jit(solution)/shard_map/ppermute | solution.py:40
  67.2 11.6 %collective-permute-start.14 = (bf16[4,144,128]{2,1,0:T(8,128)(2,1)}, bf16[4,144,128]{2,1,0:T(8,128)(2,1)S(1)}, u32[]{:S(2)}, u32[]{:S(2)}) collective-permute-start(bf16[4,144,128]{2,1,0:T(8,128)(2,1)} %get-tuple-element.23), channel_id=1, source_target_pairs={{0,2},{1,3},{2,4},{3,5},{4,6},{5,7},{6,8},{7,9},{8,10},{9,11},{10,... | collective-permute-start | bytes 442376 | tf_op jit(solution)/shard_map/ppermute | solution.py:40
  75.1 15.1 %collective-permute-start.19 = (f32[4,144,128]{2,1,0:T(8,128)S(1)}, f32[4,144,128]{2,1,0:T(8,128)S(1)}, u32[]{:S(2)}, u32[]{:S(2)}) collective-permute-start(f32[4,144,128]{2,1,0:T(8,128)S(1)} %bitcast_add_fusion.1), channel_id=1, source_target_pairs={{0,14},{1,15},{2,0},{3,1},{4,2},{5,3},{6,4},{7,5},{8,6},{9,7},{10,... | collective-permute-start | bytes 884744 | tf_op jit(solution)/shard_map/ppermute | solution.py:40
  81.2 6.6 %collective-permute-start.15 = (bf16[4,144,128]{2,1,0:T(8,128)(2,1)}, bf16[4,144,128]{2,1,0:T(8,128)(2,1)S(1)}, u32[]{:S(2)}, u32[]{:S(2)}) collective-permute-start(bf16[4,144,128]{2,1,0:T(8,128)(2,1)} %onward.6), channel_id=1, source_target_pairs={{0,2},{1,3},{2,4},{3,5},{4,6},{5,7},{6,8},{7,9},{8,10},{9,11},{10,... | collective-permute-start | bytes 442376 | tf_op jit(solution)/shard_map/ppermute | solution.py:40
  90.2 6.6 %collective-permute-start.16 = (bf16[4,144,128]{2,1,0:T(8,128)(2,1)}, bf16[4,144,128]{2,1,0:T(8,128)(2,1)S(1)}, u32[]{:S(2)}, u32[]{:S(2)}) collective-permute-start(bf16[4,144,128]{2,1,0:T(8,128)(2,1)} %onward.7), channel_id=1, source_target_pairs={{0,2},{1,3},{2,4},{3,5},{4,6},{5,7},{6,8},{7,9},{8,10},{9,11},{10,... | collective-permute-start | bytes 442376 | tf_op jit(solution)/shard_map/ppermute | solution.py:40
  91.3 14.5 %collective-permute-start.20 = (f32[4,144,128]{2,1,0:T(8,128)S(1)}, f32[4,144,128]{2,1,0:T(8,128)S(1)}, u32[]{:S(2)}, u32[]{:S(2)}) collective-permute-start(f32[4,144,128]{2,1,0:T(8,128)S(1)} %bitcast_add_fusion), channel_id=1, source_target_pairs={{0,14},{1,15},{2,0},{3,1},{4,2},{5,3},{6,4},{7,5},{8,6},{9,7},{10,... | collective-permute-start | bytes 884744 | tf_op jit(solution)/shard_map/ppermute | solution.py:40
  99.2 6.6 %collective-permute-start.17 = (bf16[4,144,128]{2,1,0:T(8,128)(2,1)}, bf16[4,144,128]{2,1,0:T(8,128)(2,1)S(1)}, u32[]{:S(2)}, u32[]{:S(2)}) collective-permute-start(bf16[4,144,128]{2,1,0:T(8,128)(2,1)} %onward.8), channel_id=1, source_target_pairs={{0,2},{1,3},{2,4},{3,5},{4,6},{5,7},{6,8},{7,9},{8,10},{9,11},{10,... | collective-permute-start | bytes 442376 | tf_op jit(solution)/shard_map/ppermute | solution.py:40
  108.6 9.8 %collective-permute-start.21 = (bf16[4,272,128]{2,1,0:T(8,128)(2,1)}, bf16[4,272,128]{2,1,0:T(8,128)(2,1)S(1)}, u32[]{:S(2)}, u32[]{:S(2)}) collective-permute-start(bf16[4,272,128]{2,1,0:T(8,128)(2,1)} %get-tuple-element.26.refs_0_), channel_id=1, source_target_pairs={{0,2},{1,3},{2,4},{3,5},{4,6},{5,7},{6,8},{7,9},{8,10},{9,11},{10,... | collective-permute-start | bytes 835592 | tf_op jit(solution)/shard_map/ppermute | solution.py:40
  108.6 9.8 %collective-permute-start.25 = (bf16[4,272,128]{2,1,0:T(8,128)(2,1)}, bf16[4,272,128]{2,1,0:T(8,128)(2,1)S(1)}, u32[]{:S(2)}, u32[]{:S(2)}) collective-permute-start(bf16[4,272,128]{2,1,0:T(8,128)(2,1)} %get-tuple-element.26.refs_0_), channel_id=1, source_target_pairs={{0,14},{1,15},{2,0},{3,1},{4,2},{5,3},{6,4},{7,5},{8,6},{9,7},{10,... | collective-permute-start | bytes 835592 | tf_op jit(solution)/shard_map/ppermute | solution.py:40
  118.4 20.6 %copy-start.3 = (bf16[4,272,128]{2,1,0:T(8,128)(2,1)}, bf16[4,272,128]{2,1,0:T(8,128)(2,1)S(1)}, u32[]{:S(2)}) copy-start(bf16[4,272,128]{2,1,0:T(8,128)(2,1)S(1)} %collective-permute-done.21.refs_1_) | copy-start | bytes 835588
  118.4 10.7 %collective-permute-start.22 = (bf16[4,272,128]{2,1,0:T(8,128)(2,1)S(1)}, bf16[4,272,128]{2,1,0:T(8,128)(2,1)S(1)}, u32[]{:S(2)}, u32[]{:S(2)}) collective-permute-start(bf16[4,272,128]{2,1,0:T(8,128)(2,1)S(1)} %collective-permute-done.21.refs_1_), channel_id=1, source_target_pairs={{0,2},{1,3},{2,4},{3,5},{4,6},{5,7},{6,8},{7,9},{8,10},{9,11},{10,... | collective-permute-start | bytes 835592 | tf_op jit(solution)/shard_map/ppermute | solution.py:40
  118.4 20.6 %copy-start.4 = (bf16[4,272,128]{2,1,0:T(8,128)(2,1)}, bf16[4,272,128]{2,1,0:T(8,128)(2,1)S(1)}, u32[]{:S(2)}) copy-start(bf16[4,272,128]{2,1,0:T(8,128)(2,1)S(1)} %collective-permute-done.25.refs_3_.refs_7_) | copy-start | bytes 835588
  118.4 10.7 %collective-permute-start.26 = (bf16[4,272,128]{2,1,0:T(8,128)(2,1)S(1)}, bf16[4,272,128]{2,1,0:T(8,128)(2,1)S(1)}, u32[]{:S(2)}, u32[]{:S(2)}) collective-permute-start(bf16[4,272,128]{2,1,0:T(8,128)(2,1)S(1)} %collective-permute-done.25.refs_3_.refs_7_), channel_id=1, source_target_pairs={{0,14},{1,15},{2,0},{3,1},{4,2},{5,3},{6,4},{7,5},{8,6},{9,7},{10,... | collective-permute-start | bytes 835592 | tf_op jit(solution)/shard_map/ppermute | solution.py:40
  129.1 9.9 %copy-start.5 = (bf16[4,272,128]{2,1,0:T(8,128)(2,1)}, bf16[4,272,128]{2,1,0:T(8,128)(2,1)S(1)}, u32[]{:S(2)}) copy-start(bf16[4,272,128]{2,1,0:T(8,128)(2,1)S(1)} %collective-permute-done.22.refs_2_) | copy-start | bytes 835588
  129.1 9.9 %collective-permute-start.23 = (bf16[4,272,128]{2,1,0:T(8,128)(2,1)S(1)}, bf16[4,272,128]{2,1,0:T(8,128)(2,1)S(1)}, u32[]{:S(2)}, u32[]{:S(2)}) collective-permute-start(bf16[4,272,128]{2,1,0:T(8,128)(2,1)S(1)} %collective-permute-done.22.refs_2_), channel_id=1, source_target_pairs={{0,2},{1,3},{2,4},{3,5},{4,6},{5,7},{6,8},{7,9},{8,10},{9,11},{10,... | collective-permute-start | bytes 835592 | tf_op jit(solution)/shard_map/ppermute | solution.py:40
  129.1 17.6 %copy-start.6 = (bf16[4,272,128]{2,1,0:T(8,128)(2,1)}, bf16[4,272,128]{2,1,0:T(8,128)(2,1)S(1)}, u32[]{:S(2)}) copy-start(bf16[4,272,128]{2,1,0:T(8,128)(2,1)S(1)} %collective-permute-done.26.refs_0_.refs_6_) | copy-start | bytes 835588
  129.1 12.3 %collective-permute-start.27 = (bf16[4,272,128]{2,1,0:T(8,128)(2,1)S(1)}, bf16[4,272,128]{2,1,0:T(8,128)(2,1)S(1)}, u32[]{:S(2)}, u32[]{:S(2)}) collective-permute-start(bf16[4,272,128]{2,1,0:T(8,128)(2,1)S(1)} %collective-permute-done.26.refs_0_.refs_6_), channel_id=1, source_target_pairs={{0,14},{1,15},{2,0},{3,1},{4,2},{5,3},{6,4},{7,5},{8,6},{9,7},{10,... | collective-permute-start | bytes 835592 | tf_op jit(solution)/shard_map/ppermute | solution.py:40
  139.0 7.8 %collective-permute-start.24 = (bf16[4,272,128]{2,1,0:T(8,128)(2,1)S(1)}, bf16[4,272,128]{2,1,0:T(8,128)(2,1)S(1)}, u32[]{:S(2)}, u32[]{:S(2)}) collective-permute-start(bf16[4,272,128]{2,1,0:T(8,128)(2,1)S(1)} %collective-permute-done.23.refs_2_.refs_3_), channel_id=1, source_target_pairs={{0,2},{1,3},{2,4},{3,5},{4,6},{5,7},{6,8},{7,9},{8,10},{9,11},{10,... | collective-permute-start | bytes 835592 | tf_op jit(solution)/shard_map/ppermute | solution.py:40
  141.4 8.4 %collective-permute-start.28 = (bf16[4,4,272,128]{3,2,1,0:T(8,128)(2,1)}, bf16[4,4,272,128]{3,2,1,0:T(8,128)(2,1)S(1)}, u32[]{:S(2)}, u32[]{:S(2)}) collective-permute-start(bf16[4,4,272,128]{3,2,1,0:T(8,128)(2,1)} %stack.42), channel_id=1, source_target_pairs={{0,1},{1,0},{2,3},{3,2},{4,5},{5,4},{6,7},{7,6},{8,9},{9,8},{10,11... | collective-permute-start | bytes 3342344 | tf_op jit(solution)/shard_map/ppermute | solution.py:35
  149.7 3.0 %collective-permute-start.29 = (bf16[4,4,272,128]{3,2,1,0:T(8,128)(2,1)}, bf16[4,4,272,128]{3,2,1,0:T(8,128)(2,1)S(1)}, u32[]{:S(2)}, u32[]{:S(2)}) collective-permute-start(bf16[4,4,272,128]{3,2,1,0:T(8,128)(2,1)} %stack.43), channel_id=1, source_target_pairs={{0,1},{1,0},{2,3},{3,2},{4,5},{5,4},{6,7},{7,6},{8,9},{9,8},{10,11... | collective-permute-start | bytes 3342344 | tf_op jit(solution)/shard_map/ppermute | solution.py:35
  176.7 3.0 %collective-permute-start.30 = (bf16[8,4,128,128]{3,2,1,0:T(8,128)(2,1)}, bf16[8,4,128,128]{3,2,1,0:T(8,128)(2,1)S(1)}, u32[]{:S(2)}, u32[]{:S(2)}) collective-permute-start(bf16[8,4,128,128]{3,2,1,0:T(8,128)(2,1)} %get-tuple-element.30), channel_id=1, source_target_pairs={{0,1},{1,0},{2,3},{3,2},{4,5},{5,4},{6,7},{7,6},{8,9},{9,8},{10,11... | collective-permute-start | bytes 3145736 | tf_op jit(solution)/shard_map/ppermute | solution.py:35
  182.7 7.0 %collective-permute-start.31 = (bf16[4,128,128]{2,1,0:T(8,128)(2,1)}, bf16[4,128,128]{2,1,0:T(8,128)(2,1)S(1)}, u32[]{:S(2)}, u32[]{:S(2)}) collective-permute-start(bf16[4,128,128]{2,1,0:T(8,128)(2,1)} %get-tuple-element.32), channel_id=1, source_target_pairs={{0,2},{1,3},{2,4},{3,5},{4,6},{5,7},{6,8},{7,9},{8,10},{9,11},{10,... | collective-permute-start | bytes 393224 | tf_op jit(solution)/shard_map/ppermute | solution.py:40
  182.7 9.4 %collective-permute-start.35 = (bf16[4,128,128]{2,1,0:T(8,128)(2,1)}, bf16[4,128,128]{2,1,0:T(8,128)(2,1)S(1)}, u32[]{:S(2)}, u32[]{:S(2)}) collective-permute-start(bf16[4,128,128]{2,1,0:T(8,128)(2,1)} %get-tuple-element.33), channel_id=1, source_target_pairs={{0,14},{1,15},{2,0},{3,1},{4,2},{5,3},{6,4},{7,5},{8,6},{9,7},{10,... | collective-permute-start | bytes 393224 | tf_op jit(solution)/shard_map/ppermute | solution.py:40
  192.1 6.4 %collective-permute-start.32 = (bf16[4,128,128]{2,1,0:T(8,128)(2,1)}, bf16[4,128,128]{2,1,0:T(8,128)(2,1)S(1)}, u32[]{:S(2)}, u32[]{:S(2)}) collective-permute-start(bf16[4,128,128]{2,1,0:T(8,128)(2,1)} %onward.9), channel_id=1, source_target_pairs={{0,2},{1,3},{2,4},{3,5},{4,6},{5,7},{6,8},{7,9},{8,10},{9,11},{10,... | collective-permute-start | bytes 393224 | tf_op jit(solution)/shard_map/ppermute | solution.py:40
  193.1 7.8 %collective-permute-start.36 = (bf16[4,128,128]{2,1,0:T(8,128)(2,1)S(1)}, bf16[4,128,128]{2,1,0:T(8,128)(2,1)S(1)}, u32[]{:S(2)}, u32[]{:S(2)}) collective-permute-start(bf16[4,128,128]{2,1,0:T(8,128)(2,1)S(1)} %fusion.1), channel_id=1, source_target_pairs={{0,14},{1,15},{2,0},{3,1},{4,2},{5,3},{6,4},{7,5},{8,6},{9,7},{10,... | collective-permute-start | bytes 393224 | tf_op jit(solution)/shard_map/ppermute | solution.py:40
  200.9 6.4 %collective-permute-start.33 = (bf16[4,128,128]{2,1,0:T(8,128)(2,1)}, bf16[4,128,128]{2,1,0:T(8,128)(2,1)S(1)}, u32[]{:S(2)}, u32[]{:S(2)}) collective-permute-start(bf16[4,128,128]{2,1,0:T(8,128)(2,1)} %onward.10), channel_id=1, source_target_pairs={{0,2},{1,3},{2,4},{3,5},{4,6},{5,7},{6,8},{7,9},{8,10},{9,11},{10,... | collective-permute-start | bytes 393224 | tf_op jit(solution)/shard_map/ppermute | solution.py:40
  201.9 9.9 %collective-permute-start.37 = (bf16[4,128,128]{2,1,0:T(8,128)(2,1)S(1)}, bf16[4,128,128]{2,1,0:T(8,128)(2,1)S(1)}, u32[]{:S(2)}, u32[]{:S(2)}) collective-permute-start(bf16[4,128,128]{2,1,0:T(8,128)(2,1)S(1)} %fusion), channel_id=1, source_target_pairs={{0,14},{1,15},{2,0},{3,1},{4,2},{5,3},{6,4},{7,5},{8,6},{9,7},{10,... | collective-permute-start | bytes 393224 | tf_op jit(solution)/shard_map/ppermute | solution.py:40
  209.6 6.4 %collective-permute-start.34 = (bf16[4,128,128]{2,1,0:T(8,128)(2,1)}, bf16[4,128,128]{2,1,0:T(8,128)(2,1)S(1)}, u32[]{:S(2)}, u32[]{:S(2)}) collective-permute-start(bf16[4,128,128]{2,1,0:T(8,128)(2,1)} %onward.11), channel_id=1, source_target_pairs={{0,2},{1,3},{2,4},{3,5},{4,6},{5,7},{6,8},{7,9},{8,10},{9,11},{10,... | collective-permute-start | bytes 393224 | tf_op jit(solution)/shard_map/ppermute | solution.py:40
  (23 other events, 42.4 us)
where the time goes:
time: 222 us; the launch traced here: 219 us
  waiting for transfers between devices  85.6 us (39%)
  Pallas kernels  61.6 us (28%)
  starting transfers between devices  52.2 us (24%)
  local copies, waits for them, and re-layouts  12.2 us (5%)
  other arithmetic  5.98 us (3%)
    ppermute x21, waiting for transfers between devices, along_z(): return lax.ppermute(v, 'pcol', [(i, (i + CORES * k) % n) for i in range(n)])  59.1 us
    ppermute x21, starting transfers between devices, along_z(): return lax.ppermute(v, 'pcol', [(i, (i + CORES * k) % n) for i in range(n)])  32.8 us
    pallas_call x1, Pallas kernels, per_device(): pl.pallas_call(project_kernel(tiles, columns), out_shape=[jax.ShapeDtypeS...  23 us
    pallas_call x1, Pallas kernels, per_device(): pl.pallas_call(sample_kernel(tiles, columns), out_shape=[jax.ShapeDtypeSt...  13 us
    unnamed x69, local copies, waits for them, and re-layouts  12.2 us
    ppermute x7, starting transfers between devices, along_y(): lax.ppermute(v, 'prow', [(SIDE * x + y, SIDE * x + (y + d) % SIDE) for x...  10.9 us
    pallas_call x6, Pallas kernels, onward(): pl.pallas_call(kernel, grid=(1,), in_specs=[plain, block(shape, k), block...  10.6 us
    ppermute x6, waiting for transfers between devices, along_x(): lax.ppermute(v, 'prow', [(SIDE * x + y, SIDE * ((x + d) % SIDE) + y) for...  9.36 us
  transfers between devices with their start and end apart: 38, of which 20 were waited for; matrix products, arithmetic and copies ran while one was open for 3% of the time, Pallas kernels for 8%

commit v1 on v0

--- a/solution.py
+++ b/solution.py
@@ -74,23 +74,30 @@
         if step < CHIPS // 2 - 1:
             down.append(along_z(down[-1], -1))
     first = to_sibling(stack(up[0], up[1], up[2], down[1]))
-    second = to_sibling(stack(down[2], down[3], up[3], up[4]))
-    return up + down[:0:-1] + [first, second]
-
-
-SIDE_ORDER = ((0, 1, 2, -1), (-2, -3, 3, 4))
+    second = to_sibling(stack(down[2], down[3], up[3]))
+    return up + down[:0:-1] + [first, second, to_sibling(up[4][None])]
+
+
+SIDE_ORDER = ((0, 1, 2, -1), (-2, -3, 3), (4,))
 
 
 def scatter_line(keep, send, down_type, few):
     other = to_sibling(send)
     half = CHIPS // 2
-    up, down, own = begin(keep, other, few, down_type)
+
+    def share(k):
+        return keep[k] + other[k].astype(F32)
+
+    if few:
+        up, down, own = begin(keep, other, few, down_type)
+    else:
+        up, down, own = share(half).astype(BF), share(half + 1).astype(down_type), share(0)
     for k in range(half - 1, 0, -1):
-        up = onward(along_z(up, 1), keep, other, k, few)
+        up = along_z(up, 1)
+        up = onward(up, keep, other, k, few) if few else (up.astype(F32) + share(k)).astype(BF)
         down = along_z(down, -1)
         if k > 1:
-            share = keep[CHIPS - k + 1] + other[CHIPS - k + 1].astype(F32)
-            down = (down.astype(F32) + share).astype(down_type)
+            down = (down.astype(F32) + share(CHIPS - k + 1)).astype(down_type)
     return own, along_z(up, 1), down
 
 
@@ -345,7 +352,7 @@
 def project_kernel(tiles, columns):
     def kernel(q_ref, left_hbm, coupling, tright, pivot, wide, *refs):
         line_pieces, refs = refs[:CHIPS], refs[CHIPS:]
-        side_pieces, refs = refs[:2], refs[2:]
+        side_pieces, refs = refs[: len(SIDE_ORDER)], refs[len(SIDE_ORDER) :]
         exact, gram, keep, send, whole, target, share, flipped, result, left, done = refs
         copy = pltpu.make_async_copy(left_hbm, left, done)
         copy.start()
@@ -469,7 +476,7 @@
             jax.ShapeDtypeStruct(share, F32),
             jax.ShapeDtypeStruct(share, BF),
         ],
-        in_specs=smem(1) + anywhere(1) + vmem(4 + CHIPS + 2),
+        in_specs=smem(1) + anywhere(1) + vmem(4 + CHIPS + len(SIDE_ORDER)),
         scratch_shapes=[
             pltpu.VMEM((tiles, order, rank), BF),
             pltpu.VMEM((tiles, order, rank), BF),

time: 222 us -> 214 us (0.964)
  Pallas kernels: 61.6 us -> 54.2 us
  waiting for transfers between devices: 85.6 us -> 92.3 us
  starting transfers between devices: 52.2 us -> 45.9 us
    ppermute x21, waiting for transfers between devices: 59.1 us -> 67.2 us  [along_z(): return lax.ppermute(v, 'pcol', [(i, (i + CORES * k) % n) for i in range(n)])]
    ppermute x21, starting transfers between devices: 32.8 us -> 26.4 us  [along_z(): return lax.ppermute(v, 'pcol', [(i, (i + CORES * k) % n) for i in range(n)])]
    pallas_call x6 -> x3, Pallas kernels: 10.6 us -> 5.34 us  [onward(): pl.pallas_call(kernel, grid=(1,), in_specs=[plain, block(shape, k), block...]
    unnamed x69 -> x65, local copies, waits for them, and re-layouts: 12.2 us -> 10.3 us
    ppermute x4 -> x5, waiting for transfers between devices: 8.76 us -> 7.37 us  [to_sibling(): return lax.ppermute(v, 'pcol', [(i, i ^ 1) for i in range(CHIPS * CORES)])]
  transfers between devices with their start and end apart: 38 -> 39, of which waited for: 20 -> 24; matrix products, arithmetic and copies ran while one was open for 3% -> 3% of each run, Pallas kernels for 8% -> 6%
where the time goes in v1:
time: 214 us; the launch traced here: 211 us
  waiting for transfers between devices  92.3 us (43%)
  Pallas kernels  54.2 us (25%)
  starting transfers between devices  45.9 us (21%)
  local copies, waits for them, and re-layouts  10.3 us (5%)
  other arithmetic  6.99 us (3%)
    ppermute x21, waiting for transfers between devices, along_z(): return lax.ppermute(v, 'pcol', [(i, (i + CORES * k) % n) for i in range(n)])  67.2 us
    ppermute x21, starting transfers between devices, along_z(): return lax.ppermute(v, 'pcol', [(i, (i + CORES * k) % n) for i in range(n)])  26.4 us
    pallas_call x1, Pallas kernels, per_device(): pl.pallas_call(project_kernel(tiles, columns), out_shape=[jax.ShapeDtypeS...  23.1 us
    pallas_call x1, Pallas kernels, per_device(): pl.pallas_call(sample_kernel(tiles, columns), out_shape=[jax.ShapeDtypeSt...  13 us
    ppermute x7, starting transfers between devices, along_y(): lax.ppermute(v, 'prow', [(SIDE * x + y, SIDE * x + (y + d) % SIDE) for x...  10.9 us
    unnamed x65, local copies, waits for them, and re-layouts  10.3 us
    ppermute x6, waiting for transfers between devices, along_x(): lax.ppermute(v, 'prow', [(SIDE * x + y, SIDE * ((x + d) % SIDE) + y) for...  9.35 us
    ppermute x7, waiting for transfers between devices, along_y(): lax.ppermute(v, 'prow', [(SIDE * x + y, SIDE * x + (y + d) % SIDE) for x...  8.34 us
  transfers between devices with their start and end apart: 39, of which 24 were waited for; matrix products, arithmetic and copies ran while one was open for 3% of the time, Pallas kernels for 6%

profile of v1, /device:TPU:6, one launch (start us, length us, event | category | flops | bytes accessed | tf_op | source)
XLA Modules:
  0.0 210.6 jit_solution(3046040713109439956)
XLA Ops:
  1.6 1.5 collective-permute-start.7
  3.1 2.1 collective-permute-start.6
  5.2 3.3 %collective-permute-done.7 = bf16[3,128,128]{2,1,0:T(8,128)(2,1)S(1)} collective-permute-done((bf16[3,128,128]{2,1,0:T(8,128)(2,1)S(1)}, bf16[3,128,128]{2,1,0:T(8,128)(2,1)S(1)}, u32[]{:S(2)}, u32[]{:S(2)}) %collective-permute-start.7) | collective-permute-done | bytes 98336 | tf_op jit(solution)/shard_map/ppermute | solution.py:50
  8.5 2.5 %collective-permute-done.8 = bf16[3,128,128]{2,1,0:T(8,128)(2,1)S(1)} collective-permute-done((bf16[3,128,128]{2,1,0:T(8,128)(2,1)S(1)}, bf16[3,128,128]{2,1,0:T(8,128)(2,1)S(1)}, u32[]{:S(2)}, u32[]{:S(2)}) %collective-permute-start.8) | collective-permute-done | bytes 98336 | tf_op jit(solution)/shard_map/ppermute | solution.py:50
  11.0 3.1 %collective-permute-start.11 = (bf16[4,3,128,128]{3,2,1,0:T(8,128)(2,1)S(1)}, bf16[4,3,128,128]{3,2,1,0:T(8,128)(2,1)S(1)}, u32[]{:S(2)}, u32[]{:S(2)}) collective-permute-start(bf16[4,3,128,128]{3,2,1,0:T(8,128)(2,1)S(1)} %pad_maximum_fusion.refs_4_), channel_id=1, source_target_pairs={{0,48},{16,0},{32,16},{48,32},{64,112},{80,64},{96,80},{112,96},{1... | collective-permute-start | bytes 1179656 | tf_op jit(solution)/shard_map/ppermute | solution.py:44
  14.1 3.2 %collective-permute-start.2 = (bf16[2,128,128]{2,1,0:T(8,128)(2,1)}, bf16[2,128,128]{2,1,0:T(8,128)(2,1)S(1)}, u32[]{:S(2)}, u32[]{:S(2)}) collective-permute-start(bf16[2,128,128]{2,1,0:T(8,128)(2,1)} %param.11), channel_id=1, source_target_pairs={{0,48},{16,0},{32,16},{48,32},{64,112},{80,64},{96,80},{112,96},{1... | collective-permute-start | bytes 196616 | tf_op jit(solution)/shard_map/ppermute | solution.py:44
  18.3 2.9 %collective-permute-done = bf16[2,128,128]{2,1,0:T(8,128)(2,1)S(1)} collective-permute-done((bf16[2,128,128]{2,1,0:T(8,128)(2,1)}, bf16[2,128,128]{2,1,0:T(8,128)(2,1)S(1)}, u32[]{:S(2)}, u32[]{:S(2)}) %collective-permute-start) | collective-permute-done | bytes 65568 | tf_op jit(solution)/shard_map/ppermute | solution.py:44
  21.2 5.4 %collective-permute-done.2 = bf16[2,128,128]{2,1,0:T(8,128)(2,1)S(1)} collective-permute-done((bf16[2,128,128]{2,1,0:T(8,128)(2,1)}, bf16[2,128,128]{2,1,0:T(8,128)(2,1)S(1)}, u32[]{:S(2)}, u32[]{:S(2)}) %collective-permute-start.2) | collective-permute-done | bytes 65568 | tf_op jit(solution)/shard_map/ppermute | solution.py:44
  27.6 2.1 collective-permute-start.4
  29.7 2.5 %collective-permute-start.3 = (bf16[4,2,128,128]{3,2,1,0:T(8,128)(2,1)S(1)}, bf16[4,2,128,128]{3,2,1,0:T(8,128)(2,1)S(1)}, u32[]{:S(2)}, u32[]{:S(2)}) collective-permute-start(bf16[4,2,128,128]{3,2,1,0:T(8,128)(2,1)S(1)} %pad_maximum_fusion.1.refs_0_), channel_id=1, source_target_pairs={{0,64},{16,80},{32,96},{48,112},{64,128},{80,144},{96,160},{112,17... | collective-permute-start | bytes 786440 | tf_op jit(solution)/shard_map/ppermute | solution.py:50
  32.3 3.7 %collective-permute-start.12 = (bf16[4,2,128,128]{3,2,1,0:T(8,128)(2,1)S(1)}, bf16[4,2,128,128]{3,2,1,0:T(8,128)(2,1)S(1)}, u32[]{:S(2)}, u32[]{:S(2)}) collective-permute-start(bf16[4,2,128,128]{3,2,1,0:T(8,128)(2,1)S(1)} %slice.89), channel_id=1, source_target_pairs={{0,48},{16,0},{32,16},{48,32},{64,112},{80,64},{96,80},{112,96},{1... | collective-permute-start | bytes 786440 | tf_op jit(solution)/shard_map/ppermute | solution.py:44
  37.3 3.5 %collective-permute-done.5.refs_3_ = bf16[4,2,128,128]{3,2,1,0:T(8,128)(2,1)S(1)} collective-permute-done((bf16[4,2,128,128]{3,2,1,0:T(8,128)(2,1)S(1)}, bf16[4,2,128,128]{3,2,1,0:T(8,128)(2,1)S(1)}, u32[]{:S(2)}, u32[]{:S(2)}) %collective-permute-start.5) | collective-permute-done | bytes 262176 | tf_op jit(solution)/shard_map/ppermute | solution.py:50
  42.0 13.0 %sample.1 = (f32[4,2,128,128]{3,2,1,0:T(8,128)}, f32[8,4,144,128]{3,2,1,0:T(8,128)}, bf16[8,4,144,128]{3,2,1,0:T(8,128)(2,1)}, bf16[2,2048,128]{2,1,0:T(8,128)(2,1)}) custom-call(s32[1]{0:T(128)} %bitcast.1.p_ref, s32[1]{0:T(128)} %bitcast.q_ref, s32[4,2]{1,0:T(4,128)} %copy.11.ranks, bf16[4,2,2048,128]{3,2,1,0:T(8,128)(2,1)} %left_hbm.3, ...), custom_call_target="tpu_custom_call" | custom-call | tf_op jit(solution)/shard_map/sample/pallas_call | solution.py:438
  55.1 3.0 %collective-permute-done.13.o0.o1.o2 = bf16[8,4,144,128]{3,2,1,0:T(8,128)(2,1)S(1)} collective-permute-done((bf16[8,4,144,128]{3,2,1,0:T(8,128)(2,1)}, bf16[8,4,144,128]{3,2,1,0:T(8,128)(2,1)S(1)}, u32[]{:S(2)}, u32[]{:S(2)}) %collective-permute-start.13) | collective-permute-done | bytes 1179680 | tf_op jit(solution)/shard_map/ppermute | solution.py:35
  59.2 2.2 %begin.1 = (bf16[4,144,128]{2,1,0:T(8,128)(2,1)}, f32[4,144,128]{2,1,0:T(8,128)}, f32[4,144,128]{2,1,0:T(8,128)}) custom-call(f32[8,4,144,128]{3,2,1,0:T(8,128)} %get-tuple-element.17.k0.k1.k2, f32[8,4,144,128]{3,2,1,0:T(8,128)} %get-tuple-element.17.k0.k1.k2, f32[8,4,144,128]{3,2,1,0:T(8,128)} %get-tuple-element.17.k0.k1.k2, ...), custom_call_target="tpu_custom_call" | custom-call | tf_op jit(solution)/shard_map/begin/pallas_call | solution.py:129
  61.4 5.9 %collective-permute-start.18 = (f32[4,144,128]{2,1,0:T(8,128)}, f32[4,144,128]{2,1,0:T(8,128)S(1)}, u32[]{:S(2)}, u32[]{:S(2)}) collective-permute-start(f32[4,144,128]{2,1,0:T(8,128)} %get-tuple-element.21), channel_id=1, source_target_pairs={{0,14},{1,15},{2,0},{3,1},{4,2},{5,3},{6,4},{7,5},{8,6},{9,7},{10,... | collective-permute-start | bytes 884744 | tf_op jit(solution)/shard_map/ppermute | solution.py:40
  67.2 6.9 %collective-permute-done.18 = f32[4,144,128]{2,1,0:T(8,128)S(1)} collective-permute-done((f32[4,144,128]{2,1,0:T(8,128)}, f32[4,144,128]{2,1,0:T(8,128)S(1)}, u32[]{:S(2)}, u32[]{:S(2)}) %collective-permute-start.18) | collective-permute-done | bytes 294944 | tf_op jit(solution)/shard_map/ppermute | solution.py:40
  75.2 3.7 %collective-permute-start.19 = (f32[4,144,128]{2,1,0:T(8,128)S(1)}, f32[4,144,128]{2,1,0:T(8,128)S(1)}, u32[]{:S(2)}, u32[]{:S(2)}) collective-permute-start(f32[4,144,128]{2,1,0:T(8,128)S(1)} %bitcast_add_fusion.1), channel_id=1, source_target_pairs={{0,14},{1,15},{2,0},{3,1},{4,2},{5,3},{6,4},{7,5},{8,6},{9,7},{10,... | collective-permute-start | bytes 884744 | tf_op jit(solution)/shard_map/ppermute | solution.py:40
  79.5 1.8 onward.3
  81.3 6.6 %collective-permute-done.15.g = bf16[4,144,128]{2,1,0:T(8,128)(2,1)S(1)} collective-permute-done((bf16[4,144,128]{2,1,0:T(8,128)(2,1)}, bf16[4,144,128]{2,1,0:T(8,128)(2,1)S(1)}, u32[]{:S(2)}, u32[]{:S(2)}) %collective-permute-start.15) | collective-permute-done | bytes 147488 | tf_op jit(solution)/shard_map/ppermute | solution.py:40
  88.5 1.8 onward.4
  91.3 3.3 %collective-permute-start.20 = (f32[4,144,128]{2,1,0:T(8,128)S(1)}, f32[4,144,128]{2,1,0:T(8,128)S(1)}, u32[]{:S(2)}, u32[]{:S(2)}) collective-permute-start(f32[4,144,128]{2,1,0:T(8,128)S(1)} %bitcast_add_fusion), channel_id=1, source_target_pairs={{0,14},{1,15},{2,0},{3,1},{4,2},{5,3},{6,4},{7,5},{8,6},{9,7},{10,... | collective-permute-start | bytes 884744 | tf_op jit(solution)/shard_map/ppermute | solution.py:40
  94.7 2.2 %collective-permute-done.16.g = bf16[4,144,128]{2,1,0:T(8,128)(2,1)S(1)} collective-permute-done((bf16[4,144,128]{2,1,0:T(8,128)(2,1)}, bf16[4,144,128]{2,1,0:T(8,128)(2,1)S(1)}, u32[]{:S(2)}, u32[]{:S(2)}) %collective-permute-start.16) | collective-permute-done | bytes 147488 | tf_op jit(solution)/shard_map/ppermute | solution.py:40
  97.5 1.8 onward.5
  100.0 5.9 %collective-permute-done.17.up = bf16[4,144,128]{2,1,0:T(8,128)(2,1)S(1)} collective-permute-done((bf16[4,144,128]{2,1,0:T(8,128)(2,1)}, bf16[4,144,128]{2,1,0:T(8,128)(2,1)S(1)}, u32[]{:S(2)}, u32[]{:S(2)}) %collective-permute-start.17) | collective-permute-done | bytes 147488 | tf_op jit(solution)/shard_map/ppermute | solution.py:40
  106.6 2.0 samples_sum.1
  108.6 2.0 collective-permute-start.21
  110.7 7.7 %collective-permute-done.25.refs_3_.refs_7_ = bf16[4,272,128]{2,1,0:T(8,128)(2,1)S(1)} collective-permute-done((bf16[4,272,128]{2,1,0:T(8,128)(2,1)}, bf16[4,272,128]{2,1,0:T(8,128)(2,1)S(1)}, u32[]{:S(2)}, u32[]{:S(2)}) %collective-permute-start.25) | collective-permute-done | bytes 278560 | tf_op jit(solution)/shard_map/ppermute | solution.py:40
  118.4 2.0 collective-permute-start.22
  120.4 6.6 %collective-permute-done.26.refs_0_.refs_6_ = bf16[4,272,128]{2,1,0:T(8,128)(2,1)S(1)} collective-permute-done((bf16[4,272,128]{2,1,0:T(8,128)(2,1)S(1)}, bf16[4,272,128]{2,1,0:T(8,128)(2,1)S(1)}, u32[]{:S(2)}, u32[]{:S(2)}) %collective-permute-start.26) | collective-permute-done | bytes 278560 | tf_op jit(solution)/shard_map/ppermute | solution.py:40
  127.0 2.0 collective-permute-start.27
  129.9 2.3 %stack.42 = bf16[4,4,272,128]{3,2,1,0:T(8,128)(2,1)} custom-call(bf16[4,272,128]{2,1,0:T(8,128)(2,1)} %get-tuple-element.23.refs_0_, bf16[4,272,128]{2,1,0:T(8,128)(2,1)} %copy-done.4, bf16[4,272,128]{2,1,0:T(8,128)(2,1)} %copy-done.6, bf16[4,272,128]{2,1,0:T(8,128)(2,1)} %copy-done.3), custom_call_target="tpu_custom_call" | custom-call | tf_op jit(solution)/shard_map/stack/pallas_call | solution.py:163
  132.2 1.4 collective-permute-done.27.refs_1_.refs_5_
  133.6 3.4 %collective-permute-done.23.refs_2_.refs_3_ = bf16[4,272,128]{2,1,0:T(8,128)(2,1)S(1)} collective-permute-done((bf16[4,272,128]{2,1,0:T(8,128)(2,1)S(1)}, bf16[4,272,128]{2,1,0:T(8,128)(2,1)S(1)}, u32[]{:S(2)}, u32[]{:S(2)}) %collective-permute-start.23) | collective-permute-done | bytes 278560 | tf_op jit(solution)/shard_map/ppermute | solution.py:40
  137.7 2.1 stack.43
  139.8 10.5 %collective-permute-done.24.refs_4_ = bf16[4,272,128]{2,1,0:T(8,128)(2,1)S(1)} collective-permute-done((bf16[4,272,128]{2,1,0:T(8,128)(2,1)}, bf16[4,272,128]{2,1,0:T(8,128)(2,1)S(1)}, u32[]{:S(2)}, u32[]{:S(2)}) %collective-permute-start.24) | collective-permute-done | bytes 278560 | tf_op jit(solution)/shard_map/ppermute | solution.py:40
  150.3 1.6 collective-permute-done.30.refs_10_
  153.2 23.1 %project.1 = (f32[4,128,128]{2,1,0:T(8,128)}, f32[4,128,128]{2,1,0:T(8,128)}, f32[8,4,128,128]{3,2,1,0:T(8,128)}, bf16[8,4,128,128]{3,2,1,0:T(8,128)(2,1)}) custom-call(s32[1]{0:T(128)} %bitcast.q_ref, bf16[4,2,2048,128]{3,2,1,0:T(8,128)(2,1)} %left_hbm.3, f32[4,2,128,128]{3,2,1,0:T(8,128)} %get-tuple-element.15.coupling, bf16[4,128,128]{2,1,0:T(8,128)(2,1)} %bitcast.50, ...), custom_call_target="tpu_custom_call" | custom-call | tf_op jit(solution)/shard_map/project/pallas_call | solution.py:471
  176.5 2.8 %collective-permute-done.31 = bf16[8,4,128,128]{3,2,1,0:T(8,128)(2,1)S(1)} collective-permute-done((bf16[8,4,128,128]{3,2,1,0:T(8,128)(2,1)}, bf16[8,4,128,128]{3,2,1,0:T(8,128)(2,1)S(1)}, u32[]{:S(2)}, u32[]{:S(2)}) %collective-permute-start.31) | collective-permute-done | bytes 1048608 | tf_op jit(solution)/shard_map/ppermute | solution.py:35
  179.3 1.9 fusion.6
  181.2 3.2 %collective-permute-start.36 = (bf16[4,128,128]{2,1,0:T(8,128)(2,1)S(1)}, bf16[4,128,128]{2,1,0:T(8,128)(2,1)S(1)}, u32[]{:S(2)}, u32[]{:S(2)}) collective-permute-start(bf16[4,128,128]{2,1,0:T(8,128)(2,1)S(1)} %get-tuple-element.32), channel_id=1, source_target_pairs={{0,14},{1,15},{2,0},{3,1},{4,2},{5,3},{6,4},{7,5},{8,6},{9,7},{10,... | collective-permute-start | bytes 393224 | tf_op jit(solution)/shard_map/ppermute | solution.py:40
  184.4 3.5 %collective-permute-done.32 = bf16[4,128,128]{2,1,0:T(8,128)(2,1)S(1)} collective-permute-done((bf16[4,128,128]{2,1,0:T(8,128)(2,1)S(1)}, bf16[4,128,128]{2,1,0:T(8,128)(2,1)S(1)}, u32[]{:S(2)}, u32[]{:S(2)}) %collective-permute-start.32) | collective-permute-done | bytes 131104 | tf_op jit(solution)/shard_map/ppermute | solution.py:40
  189.0 6.2 %collective-permute-done.33 = bf16[4,128,128]{2,1,0:T(8,128)(2,1)S(1)} collective-permute-done((bf16[4,128,128]{2,1,0:T(8,128)(2,1)S(1)}, bf16[4,128,128]{2,1,0:T(8,128)(2,1)S(1)}, u32[]{:S(2)}, u32[]{:S(2)}) %collective-permute-start.33) | collective-permute-done | bytes 131104 | tf_op jit(solution)/shard_map/ppermute | solution.py:40
  195.4 2.0 collective-permute-start.34
  197.4 2.9 %collective-permute-done.37 = bf16[4,128,128]{2,1,0:T(8,128)(2,1)S(1)} collective-permute-done((bf16[4,128,128]{2,1,0:T(8,128)(2,1)S(1)}, bf16[4,128,128]{2,1,0:T(8,128)(2,1)S(1)}, u32[]{:S(2)}, u32[]{:S(2)}) %collective-permute-start.37) | collective-permute-done | bytes 131104 | tf_op jit(solution)/shard_map/ppermute | solution.py:40
  201.8 2.0 collective-permute-start.35
  203.8 2.2 %basis.1 = f32[128,4,128]{2,1,0:T(4,128)} custom-call(f32[4,128,128]{2,1,0:T(8,128)} %get-tuple-element.24.exact, f32[4,128,128]{2,1,0:T(8,128)} %get-tuple-element.25.inverse), custom_call_target="tpu_custom_call" | custom-call | tf_op jit(solution)/shard_map/basis/pallas_call | solution.py:491
  208.7 1.9 finish.1
  (117 shorter events, 20.6 us)
Async XLA Ops:
  0.6 35.3 %copy-start.30 = (s32[4,2]{0,1:T(2,128)S(1)}, s32[4,2]{0,1:T(2,128)}, u32[]{:S(2)}) copy-start(s32[4,2]{0,1:T(2,128)} %param.15) | copy-start | bytes 100
  0.6 36.0 %copy-start.26 = (bf16[128,4,128]{2,1,0:T(4,128)(2,1)S(1)}, bf16[128,4,128]{2,1,0:T(4,128)(2,1)}, u32[]{:S(2)}) copy-start(bf16[128,4,128]{2,1,0:T(4,128)(2,1)} %param.13) | copy-start | bytes 393220
  1.6 6.9 %collective-permute-start.7 = (bf16[3,128,128]{2,1,0:T(8,128)(2,1)S(1)}, bf16[3,128,128]{2,1,0:T(8,128)(2,1)S(1)}, u32[]{:S(2)}, u32[]{:S(2)}) collective-permute-start(bf16[3,128,128]{2,1,0:T(8,128)(2,1)S(1)} %get-tuple-element.36), channel_id=1, source_target_pairs={{0,128},{16,144},{32,160},{48,176},{64,192},{80,208},{96,224},{112... | collective-permute-start | bytes 294920 | tf_op jit(solution)/shard_map/ppermute | solution.py:50
  3.1 5.4 %collective-permute-start.6 = (bf16[3,128,128]{2,1,0:T(8,128)(2,1)S(1)}, bf16[3,128,128]{2,1,0:T(8,128)(2,1)S(1)}, u32[]{:S(2)}, u32[]{:S(2)}) collective-permute-start(bf16[3,128,128]{2,1,0:T(8,128)(2,1)S(1)} %get-tuple-element.36), channel_id=1, source_target_pairs={{0,64},{16,80},{32,96},{48,112},{64,128},{80,144},{96,160},{112,17... | collective-permute-start | bytes 294920 | tf_op jit(solution)/shard_map/ppermute | solution.py:50
  5.2 5.8 %collective-permute-start.8 = (bf16[3,128,128]{2,1,0:T(8,128)(2,1)S(1)}, bf16[3,128,128]{2,1,0:T(8,128)(2,1)S(1)}, u32[]{:S(2)}, u32[]{:S(2)}) collective-permute-start(bf16[3,128,128]{2,1,0:T(8,128)(2,1)S(1)} %get-tuple-element.36), channel_id=1, source_target_pairs={{0,192},{16,208},{32,224},{48,240},{64,0},{80,16},{96,32},{112,48}... | collective-permute-start | bytes 294920 | tf_op jit(solution)/shard_map/ppermute | solution.py:50
  11.0 29.9 %copy-start.1 = (bf16[4,3,128,128]{3,2,1,0:T(8,128)(2,1)}, bf16[4,3,128,128]{3,2,1,0:T(8,128)(2,1)S(1)}, u32[]{:S(2)}) copy-start(bf16[4,3,128,128]{3,2,1,0:T(8,128)(2,1)S(1)} %pad_maximum_fusion.refs_4_) | copy-start | bytes 1179652
  11.0 18.7 %collective-permute-start.11 = (bf16[4,3,128,128]{3,2,1,0:T(8,128)(2,1)S(1)}, bf16[4,3,128,128]{3,2,1,0:T(8,128)(2,1)S(1)}, u32[]{:S(2)}, u32[]{:S(2)}) collective-permute-start(bf16[4,3,128,128]{3,2,1,0:T(8,128)(2,1)S(1)} %pad_maximum_fusion.refs_4_), channel_id=1, source_target_pairs={{0,48},{16,0},{32,16},{48,32},{64,112},{80,64},{96,80},{112,96},{1... | collective-permute-start | bytes 1179656 | tf_op jit(solution)/shard_map/ppermute | solution.py:44
  14.1 7.1 %collective-permute-start = (bf16[2,128,128]{2,1,0:T(8,128)(2,1)}, bf16[2,128,128]{2,1,0:T(8,128)(2,1)S(1)}, u32[]{:S(2)}, u32[]{:S(2)}) collective-permute-start(bf16[2,128,128]{2,1,0:T(8,128)(2,1)} %param.11), channel_id=1, source_target_pairs={{0,16},{16,32},{32,48},{48,0},{64,80},{80,96},{96,112},{112,64},{1... | collective-permute-start | bytes 196616 | tf_op jit(solution)/shard_map/ppermute | solution.py:44
  14.1 12.5 %collective-permute-start.2 = (bf16[2,128,128]{2,1,0:T(8,128)(2,1)}, bf16[2,128,128]{2,1,0:T(8,128)(2,1)S(1)}, u32[]{:S(2)}, u32[]{:S(2)}) collective-permute-start(bf16[2,128,128]{2,1,0:T(8,128)(2,1)} %param.11), channel_id=1, source_target_pairs={{0,48},{16,0},{32,16},{48,32},{64,112},{80,64},{96,80},{112,96},{1... | collective-permute-start | bytes 196616 | tf_op jit(solution)/shard_map/ppermute | solution.py:44
  17.4 9.3 %collective-permute-start.1 = (bf16[2,128,128]{2,1,0:T(8,128)(2,1)}, bf16[2,128,128]{2,1,0:T(8,128)(2,1)S(1)}, u32[]{:S(2)}, u32[]{:S(2)}) collective-permute-start(bf16[2,128,128]{2,1,0:T(8,128)(2,1)} %param.11), channel_id=1, source_target_pairs={{0,32},{16,48},{32,0},{48,16},{64,96},{80,112},{96,64},{112,80},{1... | collective-permute-start | bytes 196616 | tf_op jit(solution)/shard_map/ppermute | solution.py:44
  17.4 23.5 %collective-permute-start.9 = (bf16[4,3,128,128]{3,2,1,0:T(8,128)(2,1)S(1)}, bf16[4,3,128,128]{3,2,1,0:T(8,128)(2,1)S(1)}, u32[]{:S(2)}, u32[]{:S(2)}) collective-permute-start(bf16[4,3,128,128]{3,2,1,0:T(8,128)(2,1)S(1)} %pad_maximum_fusion.refs_4_), channel_id=1, source_target_pairs={{0,16},{16,32},{32,48},{48,0},{64,80},{80,96},{96,112},{112,64},{1... | collective-permute-start | bytes 1179656 | tf_op jit(solution)/shard_map/ppermute | solution.py:44
  21.2 11.1 %collective-permute-start.10 = (bf16[4,1,128,128]{3,2,1,0:T(8,128)(2,1)S(1)}, bf16[4,1,128,128]{3,2,1,0:T(8,128)(2,1)S(1)}, u32[]{:S(2)}, u32[]{:S(2)}) collective-permute-start(bf16[4,1,128,128]{3,2,1,0:T(8,128)(2,1)S(1)} %slice.88), channel_id=1, source_target_pairs={{0,32},{16,48},{32,0},{48,16},{64,96},{80,112},{96,64},{112,80},{1... | collective-permute-start | bytes 393224 | tf_op jit(solution)/shard_map/ppermute | solution.py:44
  27.5 13.4 %copy-start.11 = (bf16[4,2,128,128]{3,2,1,0:T(8,128)(2,1)}, bf16[4,2,128,128]{3,2,1,0:T(8,128)(2,1)S(1)}, u32[]{:S(2)}) copy-start(bf16[4,2,128,128]{3,2,1,0:T(8,128)(2,1)S(1)} %pad_maximum_fusion.1.refs_0_) | copy-start | bytes 786436
  27.6 13.3 %collective-permute-start.5 = (bf16[4,2,128,128]{3,2,1,0:T(8,128)(2,1)S(1)}, bf16[4,2,128,128]{3,2,1,0:T(8,128)(2,1)S(1)}, u32[]{:S(2)}, u32[]{:S(2)}) collective-permute-start(bf16[4,2,128,128]{3,2,1,0:T(8,128)(2,1)S(1)} %pad_maximum_fusion.1.refs_0_), channel_id=1, source_target_pairs={{0,192},{16,208},{32,224},{48,240},{64,0},{80,16},{96,32},{112,48}... | collective-permute-start | bytes 786440 | tf_op jit(solution)/shard_map/ppermute | solution.py:50
  27.6 13.2 %collective-permute-start.4 = (bf16[4,2,128,128]{3,2,1,0:T(8,128)(2,1)S(1)}, bf16[4,2,128,128]{3,2,1,0:T(8,128)(2,1)S(1)}, u32[]{:S(2)}, u32[]{:S(2)}) collective-permute-start(bf16[4,2,128,128]{3,2,1,0:T(8,128)(2,1)S(1)} %pad_maximum_fusion.1.refs_0_), channel_id=1, source_target_pairs={{0,128},{16,144},{32,160},{48,176},{64,192},{80,208},{96,224},{112... | collective-permute-start | bytes 786440 | tf_op jit(solution)/shard_map/ppermute | solution.py:50
  29.7 11.2 %copy-start.10 = (bf16[4,3,128,128]{3,2,1,0:T(8,128)(2,1)}, bf16[4,3,128,128]{3,2,1,0:T(8,128)(2,1)S(1)}, u32[]{:S(2)}) copy-start(bf16[4,3,128,128]{3,2,1,0:T(8,128)(2,1)S(1)} %collective-permute-done.11.refs_8_) | copy-start | bytes 1179652
  29.7 11.1 %collective-permute-start.3 = (bf16[4,2,128,128]{3,2,1,0:T(8,128)(2,1)S(1)}, bf16[4,2,128,128]{3,2,1,0:T(8,128)(2,1)S(1)}, u32[]{:S(2)}, u32[]{:S(2)}) collective-permute-start(bf16[4,2,128,128]{3,2,1,0:T(8,128)(2,1)S(1)} %pad_maximum_fusion.1.refs_0_), channel_id=1, source_target_pairs={{0,64},{16,80},{32,96},{48,112},{64,128},{80,144},{96,160},{112,17... | collective-permute-start | bytes 786440 | tf_op jit(solution)/shard_map/ppermute | solution.py:50
  32.3 8.6 %collective-permute-start.12 = (bf16[4,2,128,128]{3,2,1,0:T(8,128)(2,1)S(1)}, bf16[4,2,128,128]{3,2,1,0:T(8,128)(2,1)S(1)}, u32[]{:S(2)}, u32[]{:S(2)}) collective-permute-start(bf16[4,2,128,128]{3,2,1,0:T(8,128)(2,1)S(1)} %slice.89), channel_id=1, source_target_pairs={{0,48},{16,0},{32,16},{48,32},{64,112},{80,64},{96,80},{112,96},{1... | collective-permute-start | bytes 786440 | tf_op jit(solution)/shard_map/ppermute | solution.py:44
  55.0 3.1 %collective-permute-start.13 = (bf16[8,4,144,128]{3,2,1,0:T(8,128)(2,1)}, bf16[8,4,144,128]{3,2,1,0:T(8,128)(2,1)S(1)}, u32[]{:S(2)}, u32[]{:S(2)}) collective-permute-start(bf16[8,4,144,128]{3,2,1,0:T(8,128)(2,1)} %get-tuple-element.18), channel_id=1, source_target_pairs={{0,1},{1,0},{2,3},{3,2},{4,5},{5,4},{6,7},{7,6},{8,9},{9,8},{10,11... | collective-permute-start | bytes 3538952 | tf_op jit(solution)/shard_map/ppermute | solution.py:35
  61.4 12.7 %collective-permute-start.18 = (f32[4,144,128]{2,1,0:T(8,128)}, f32[4,144,128]{2,1,0:T(8,128)S(1)}, u32[]{:S(2)}, u32[]{:S(2)}) collective-permute-start(f32[4,144,128]{2,1,0:T(8,128)} %get-tuple-element.21), channel_id=1, source_target_pairs={{0,14},{1,15},{2,0},{3,1},{4,2},{5,3},{6,4},{7,5},{8,6},{9,7},{10,... | collective-permute-start | bytes 884744 | tf_op jit(solution)/shard_map/ppermute | solution.py:40
  67.2 11.6 %collective-permute-start.14 = (bf16[4,144,128]{2,1,0:T(8,128)(2,1)}, bf16[4,144,128]{2,1,0:T(8,128)(2,1)S(1)}, u32[]{:S(2)}, u32[]{:S(2)}) collective-permute-start(bf16[4,144,128]{2,1,0:T(8,128)(2,1)} %get-tuple-element.20), channel_id=1, source_target_pairs={{0,2},{1,3},{2,4},{3,5},{4,6},{5,7},{6,8},{7,9},{8,10},{9,11},{10,... | collective-permute-start | bytes 442376 | tf_op jit(solution)/shard_map/ppermute | solution.py:40
  75.2 15.1 %collective-permute-start.19 = (f32[4,144,128]{2,1,0:T(8,128)S(1)}, f32[4,144,128]{2,1,0:T(8,128)S(1)}, u32[]{:S(2)}, u32[]{:S(2)}) collective-permute-start(f32[4,144,128]{2,1,0:T(8,128)S(1)} %bitcast_add_fusion.1), channel_id=1, source_target_pairs={{0,14},{1,15},{2,0},{3,1},{4,2},{5,3},{6,4},{7,5},{8,6},{9,7},{10,... | collective-permute-start | bytes 884744 | tf_op jit(solution)/shard_map/ppermute | solution.py:40
  81.3 6.6 %collective-permute-start.15 = (bf16[4,144,128]{2,1,0:T(8,128)(2,1)}, bf16[4,144,128]{2,1,0:T(8,128)(2,1)S(1)}, u32[]{:S(2)}, u32[]{:S(2)}) collective-permute-start(bf16[4,144,128]{2,1,0:T(8,128)(2,1)} %onward.3), channel_id=1, source_target_pairs={{0,2},{1,3},{2,4},{3,5},{4,6},{5,7},{6,8},{7,9},{8,10},{9,11},{10,... | collective-permute-start | bytes 442376 | tf_op jit(solution)/shard_map/ppermute | solution.py:40
  90.3 6.6 %collective-permute-start.16 = (bf16[4,144,128]{2,1,0:T(8,128)(2,1)}, bf16[4,144,128]{2,1,0:T(8,128)(2,1)S(1)}, u32[]{:S(2)}, u32[]{:S(2)}) collective-permute-start(bf16[4,144,128]{2,1,0:T(8,128)(2,1)} %onward.4), channel_id=1, source_target_pairs={{0,2},{1,3},{2,4},{3,5},{4,6},{5,7},{6,8},{7,9},{8,10},{9,11},{10,... | collective-permute-start | bytes 442376 | tf_op jit(solution)/shard_map/ppermute | solution.py:40
  91.3 14.5 %collective-permute-start.20 = (f32[4,144,128]{2,1,0:T(8,128)S(1)}, f32[4,144,128]{2,1,0:T(8,128)S(1)}, u32[]{:S(2)}, u32[]{:S(2)}) collective-permute-start(f32[4,144,128]{2,1,0:T(8,128)S(1)} %bitcast_add_fusion), channel_id=1, source_target_pairs={{0,14},{1,15},{2,0},{3,1},{4,2},{5,3},{6,4},{7,5},{8,6},{9,7},{10,... | collective-permute-start | bytes 884744 | tf_op jit(solution)/shard_map/ppermute | solution.py:40
  99.3 6.6 %collective-permute-start.17 = (bf16[4,144,128]{2,1,0:T(8,128)(2,1)}, bf16[4,144,128]{2,1,0:T(8,128)(2,1)S(1)}, u32[]{:S(2)}, u32[]{:S(2)}) collective-permute-start(bf16[4,144,128]{2,1,0:T(8,128)(2,1)} %onward.5), channel_id=1, source_target_pairs={{0,2},{1,3},{2,4},{3,5},{4,6},{5,7},{6,8},{7,9},{8,10},{9,11},{10,... | collective-permute-start | bytes 442376 | tf_op jit(solution)/shard_map/ppermute | solution.py:40
  108.6 9.7 %collective-permute-start.25 = (bf16[4,272,128]{2,1,0:T(8,128)(2,1)}, bf16[4,272,128]{2,1,0:T(8,128)(2,1)S(1)}, u32[]{:S(2)}, u32[]{:S(2)}) collective-permute-start(bf16[4,272,128]{2,1,0:T(8,128)(2,1)} %get-tuple-element.23.refs_0_), channel_id=1, source_target_pairs={{0,14},{1,15},{2,0},{3,1},{4,2},{5,3},{6,4},{7,5},{8,6},{9,7},{10,... | collective-permute-start | bytes 835592 | tf_op jit(solution)/shard_map/ppermute | solution.py:40
  108.6 9.8 %collective-permute-start.21 = (bf16[4,272,128]{2,1,0:T(8,128)(2,1)}, bf16[4,272,128]{2,1,0:T(8,128)(2,1)S(1)}, u32[]{:S(2)}, u32[]{:S(2)}) collective-permute-start(bf16[4,272,128]{2,1,0:T(8,128)(2,1)} %get-tuple-element.23.refs_0_), channel_id=1, source_target_pairs={{0,2},{1,3},{2,4},{3,5},{4,6},{5,7},{6,8},{7,9},{8,10},{9,11},{10,... | collective-permute-start | bytes 835592 | tf_op jit(solution)/shard_map/ppermute | solution.py:40
  118.4 10.8 %copy-start.3 = (bf16[4,272,128]{2,1,0:T(8,128)(2,1)}, bf16[4,272,128]{2,1,0:T(8,128)(2,1)S(1)}, u32[]{:S(2)}) copy-start(bf16[4,272,128]{2,1,0:T(8,128)(2,1)S(1)} %collective-permute-done.25.refs_3_.refs_7_) | copy-start | bytes 835588
  118.4 8.7 %collective-permute-start.26 = (bf16[4,272,128]{2,1,0:T(8,128)(2,1)S(1)}, bf16[4,272,128]{2,1,0:T(8,128)(2,1)S(1)}, u32[]{:S(2)}, u32[]{:S(2)}) collective-permute-start(bf16[4,272,128]{2,1,0:T(8,128)(2,1)S(1)} %collective-permute-done.25.refs_3_.refs_7_), channel_id=1, source_target_pairs={{0,14},{1,15},{2,0},{3,1},{4,2},{5,3},{6,4},{7,5},{8,6},{9,7},{10,... | collective-permute-start | bytes 835592 | tf_op jit(solution)/shard_map/ppermute | solution.py:40
  118.4 10.8 %copy-start.4 = (bf16[4,272,128]{2,1,0:T(8,128)(2,1)}, bf16[4,272,128]{2,1,0:T(8,128)(2,1)S(1)}, u32[]{:S(2)}) copy-start(bf16[4,272,128]{2,1,0:T(8,128)(2,1)S(1)} %collective-permute-done.21.refs_1_) | copy-start | bytes 835588
  118.4 10.8 %collective-permute-start.22 = (bf16[4,272,128]{2,1,0:T(8,128)(2,1)S(1)}, bf16[4,272,128]{2,1,0:T(8,128)(2,1)S(1)}, u32[]{:S(2)}, u32[]{:S(2)}) collective-permute-start(bf16[4,272,128]{2,1,0:T(8,128)(2,1)S(1)} %collective-permute-done.21.refs_1_), channel_id=1, source_target_pairs={{0,2},{1,3},{2,4},{3,5},{4,6},{5,7},{6,8},{7,9},{8,10},{9,11},{10,... | collective-permute-start | bytes 835592 | tf_op jit(solution)/shard_map/ppermute | solution.py:40
  127.0 9.9 %copy-start.5 = (bf16[4,272,128]{2,1,0:T(8,128)(2,1)}, bf16[4,272,128]{2,1,0:T(8,128)(2,1)S(1)}, u32[]{:S(2)}) copy-start(bf16[4,272,128]{2,1,0:T(8,128)(2,1)S(1)} %collective-permute-done.26.refs_0_.refs_6_) | copy-start | bytes 835588
  127.0 6.5 %collective-permute-start.27 = (bf16[4,272,128]{2,1,0:T(8,128)(2,1)S(1)}, bf16[4,272,128]{2,1,0:T(8,128)(2,1)S(1)}, u32[]{:S(2)}, u32[]{:S(2)}) collective-permute-start(bf16[4,272,128]{2,1,0:T(8,128)(2,1)S(1)} %collective-permute-done.26.refs_0_.refs_6_), channel_id=1, source_target_pairs={{0,14},{1,15},{2,0},{3,1},{4,2},{5,3},{6,4},{7,5},{8,6},{9,7},{10,... | collective-permute-start | bytes 835592 | tf_op jit(solution)/shard_map/ppermute | solution.py:40
  129.2 7.8 %collective-permute-start.23 = (bf16[4,272,128]{2,1,0:T(8,128)(2,1)S(1)}, bf16[4,272,128]{2,1,0:T(8,128)(2,1)S(1)}, u32[]{:S(2)}, u32[]{:S(2)}) collective-permute-start(bf16[4,272,128]{2,1,0:T(8,128)(2,1)S(1)} %collective-permute-done.22.refs_2_), channel_id=1, source_target_pairs={{0,2},{1,3},{2,4},{3,5},{4,6},{5,7},{6,8},{7,9},{8,10},{9,11},{10,... | collective-permute-start | bytes 835592 | tf_op jit(solution)/shard_map/ppermute | solution.py:40
  132.2 19.6 %collective-permute-start.28 = (bf16[4,4,272,128]{3,2,1,0:T(8,128)(2,1)}, bf16[4,4,272,128]{3,2,1,0:T(8,128)(2,1)S(1)}, u32[]{:S(2)}, u32[]{:S(2)}) collective-permute-start(bf16[4,4,272,128]{3,2,1,0:T(8,128)(2,1)} %stack.42), channel_id=1, source_target_pairs={{0,1},{1,0},{2,3},{3,2},{4,5},{5,4},{6,7},{7,6},{8,9},{9,8},{10,11... | collective-permute-start | bytes 3342344 | tf_op jit(solution)/shard_map/ppermute | solution.py:35
  139.8 12.1 %collective-permute-start.29 = (bf16[3,4,272,128]{3,2,1,0:T(8,128)(2,1)}, bf16[3,4,272,128]{3,2,1,0:T(8,128)(2,1)S(1)}, u32[]{:S(2)}, u32[]{:S(2)}) collective-permute-start(bf16[3,4,272,128]{3,2,1,0:T(8,128)(2,1)} %stack.43), channel_id=1, source_target_pairs={{0,1},{1,0},{2,3},{3,2},{4,5},{5,4},{6,7},{7,6},{8,9},{9,8},{10,11... | collective-permute-start | bytes 2506760 | tf_op jit(solution)/shard_map/ppermute | solution.py:35
  139.8 10.5 %collective-permute-start.24 = (bf16[4,272,128]{2,1,0:T(8,128)(2,1)}, bf16[4,272,128]{2,1,0:T(8,128)(2,1)S(1)}, u32[]{:S(2)}, u32[]{:S(2)}) collective-permute-start(bf16[4,272,128]{2,1,0:T(8,128)(2,1)} %copy-done.8), channel_id=1, source_target_pairs={{0,2},{1,3},{2,4},{3,5},{4,6},{5,7},{6,8},{7,9},{8,10},{9,11},{10,... | collective-permute-start | bytes 835592 | tf_op jit(solution)/shard_map/ppermute | solution.py:40
  150.3 1.6 collective-permute-start.30
  176.3 18.9 %copy-start.2 = (f32[8,4,128,128]{3,2,1,0:T(8,128)S(1)}, f32[8,4,128,128]{3,2,1,0:T(8,128)}, u32[]{:S(2)}) copy-start(f32[8,4,128,128]{3,2,1,0:T(8,128)} %get-tuple-element.26) | copy-start | bytes 6291460
  176.3 3.0 %collective-permute-start.31 = (bf16[8,4,128,128]{3,2,1,0:T(8,128)(2,1)}, bf16[8,4,128,128]{3,2,1,0:T(8,128)(2,1)S(1)}, u32[]{:S(2)}, u32[]{:S(2)}) collective-permute-start(bf16[8,4,128,128]{3,2,1,0:T(8,128)(2,1)} %get-tuple-element.27), channel_id=1, source_target_pairs={{0,1},{1,0},{2,3},{3,2},{4,5},{5,4},{6,7},{7,6},{8,9},{9,8},{10,11... | collective-permute-start | bytes 3145736 | tf_op jit(solution)/shard_map/ppermute | solution.py:35
  181.2 6.7 %collective-permute-start.32 = (bf16[4,128,128]{2,1,0:T(8,128)(2,1)S(1)}, bf16[4,128,128]{2,1,0:T(8,128)(2,1)S(1)}, u32[]{:S(2)}, u32[]{:S(2)}) collective-permute-start(bf16[4,128,128]{2,1,0:T(8,128)(2,1)S(1)} %get-tuple-element.33), channel_id=1, source_target_pairs={{0,2},{1,3},{2,4},{3,5},{4,6},{5,7},{6,8},{7,9},{8,10},{9,11},{10,... | collective-permute-start | bytes 393224 | tf_op jit(solution)/shard_map/ppermute | solution.py:40
  181.2 7.8 %collective-permute-start.36 = (bf16[4,128,128]{2,1,0:T(8,128)(2,1)S(1)}, bf16[4,128,128]{2,1,0:T(8,128)(2,1)S(1)}, u32[]{:S(2)}, u32[]{:S(2)}) collective-permute-start(bf16[4,128,128]{2,1,0:T(8,128)(2,1)S(1)} %get-tuple-element.32), channel_id=1, source_target_pairs={{0,14},{1,15},{2,0},{3,1},{4,2},{5,3},{6,4},{7,5},{8,6},{9,7},{10,... | collective-permute-start | bytes 393224 | tf_op jit(solution)/shard_map/ppermute | solution.py:40
  188.9 6.3 %collective-permute-start.33 = (bf16[4,128,128]{2,1,0:T(8,128)(2,1)S(1)}, bf16[4,128,128]{2,1,0:T(8,128)(2,1)S(1)}, u32[]{:S(2)}, u32[]{:S(2)}) collective-permute-start(bf16[4,128,128]{2,1,0:T(8,128)(2,1)S(1)} %fusion.4), channel_id=1, source_target_pairs={{0,2},{1,3},{2,4},{3,5},{4,6},{5,7},{6,8},{7,9},{8,10},{9,11},{10,... | collective-permute-start | bytes 393224 | tf_op jit(solution)/shard_map/ppermute | solution.py:40
  195.3 5.0 %collective-permute-start.37 = (bf16[4,128,128]{2,1,0:T(8,128)(2,1)S(1)}, bf16[4,128,128]{2,1,0:T(8,128)(2,1)S(1)}, u32[]{:S(2)}, u32[]{:S(2)}) collective-permute-start(bf16[4,128,128]{2,1,0:T(8,128)(2,1)S(1)} %get-tuple-element.30), channel_id=1, source_target_pairs={{0,14},{1,15},{2,0},{3,1},{4,2},{5,3},{6,4},{7,5},{8,6},{9,7},{10,... | collective-permute-start | bytes 393224 | tf_op jit(solution)/shard_map/ppermute | solution.py:40
  195.4 6.3 %collective-permute-start.34 = (bf16[4,128,128]{2,1,0:T(8,128)(2,1)S(1)}, bf16[4,128,128]{2,1,0:T(8,128)(2,1)S(1)}, u32[]{:S(2)}, u32[]{:S(2)}) collective-permute-start(bf16[4,128,128]{2,1,0:T(8,128)(2,1)S(1)} %get-tuple-element.31), channel_id=1, source_target_pairs={{0,2},{1,3},{2,4},{3,5},{4,6},{5,7},{6,8},{7,9},{8,10},{9,11},{10,... | collective-permute-start | bytes 393224 | tf_op jit(solution)/shard_map/ppermute | solution.py:40
  201.7 5.0 %collective-permute-start.38 = (bf16[4,128,128]{2,1,0:T(8,128)(2,1)S(1)}, bf16[4,128,128]{2,1,0:T(8,128)(2,1)S(1)}, u32[]{:S(2)}, u32[]{:S(2)}) collective-permute-start(bf16[4,128,128]{2,1,0:T(8,128)(2,1)S(1)} %get-tuple-element.28), channel_id=1, source_target_pairs={{0,14},{1,15},{2,0},{3,1},{4,2},{5,3},{6,4},{7,5},{8,6},{9,7},{10,... | collective-permute-start | bytes 393224 | tf_op jit(solution)/shard_map/ppermute | solution.py:40
  201.8 6.3 %collective-permute-start.35 = (bf16[4,128,128]{2,1,0:T(8,128)(2,1)S(1)}, bf16[4,128,128]{2,1,0:T(8,128)(2,1)S(1)}, u32[]{:S(2)}, u32[]{:S(2)}) collective-permute-start(bf16[4,128,128]{2,1,0:T(8,128)(2,1)S(1)} %get-tuple-element.29), channel_id=1, source_target_pairs={{0,2},{1,3},{2,4},{3,5},{4,6},{5,7},{6,8},{7,9},{8,10},{9,11},{10,... | collective-permute-start | bytes 393224 | tf_op jit(solution)/shard_map/ppermute | solution.py:40
  (22 other events, 36.9 us)
